TPU v7x, 32 devices: a whole 2x2x4 slice. The times are simulated.
32 devices in a mesh: az: 8 (over y, x, core), rg: 4 (over z).
Axes of the slice: x: 2, y: 2, z: 4, core: 2. Of those that a mesh axis runs over, the one named last changes fastest.
Arguments:
- reference_slc: bfloat16 [2, 768, 12288], P(None, 'az', 'rg'), may hold values from -6 to 6
- secondary_slc: bfloat16 [2, 768, 12288], P(None, 'az', 'rg'), may hold values from -6 to 6
- chip_offsets: int32 [2, 8, 384], P(None, 'az', 'rg'), may hold values from -80 to 80, as said below
- src_row: int32 [768], replicated, may hold values from 0 to 767, as said below
- line_owner: int32 [768], replicated, may hold values from 0 to 31, as said below
- band_start: int32 [12288], replicated, may hold values from -64 to 12343, as said below
- band_taps: bfloat16 [8, 12288], replicated, may hold values from -2.09375 to 2.09375
Outputs:
- est_offsets: float32 [2, 8, 384], P(None, 'az', 'rg')
- resampled: bfloat16 [2, 1024, 12288], P(None, ('az', 'rg'))
Inputs may be any that keep to these rules, and one draw needn't show every extreme that they name: chip_offsets[0] lies within -80 and 80, chip_offsets[1] within -48 and 48. `src_row`: the source row of line i lies within 8 rows of i. `line_owner`: for every owner and every azimuth tile, at most 4 lines of that owner take their source rows from that tile, and an owner holds at most 32 lines; both bounds are met in every draw. band_start[j] lies within j - 64 and j + 56.
All inputs are finite; a program needn't handle non-finite values.
Results may differ from a plain program's by a relative error of at most 0.008.
Values may be sent and summed in bfloat16 or wider, within the bound.
A program may use at most 128 MiB of HBM per device.

v0:
```python
import functools
import math

import jax
import jax.numpy as jnp
import numpy as np
from jax import lax
from jax.experimental import pallas as pl
from jax.experimental.pallas import tpu as pltpu
from jax.sharding import PartitionSpec as P

CHIP_LEN = 64
OVERSAMPLE = 16
LAG_COUNT = 48
TAP_COUNT = 8
SPACING = 32
MARGIN = 64
MAX_SHIFT = 8
LANES = 128
GROUP = 8

PHASE_RATE = 2.0
EPS = 1e-06
VMEM_LIMIT = 56 * 1024 * 1024


def shifted(cells, axis, up):
    count = lax.axis_size(axis)
    if up:
        pairs = [(i, i + 1) for i in range(count - 1)]
    else:
        pairs = [(i + 1, i) for i in range(count - 1)]
    return lax.ppermute(cells, axis, pairs)


def make_tables():
    indices = np.arange(CHIP_LEN)
    product = indices[:, None] * indices[None, :] % CHIP_LEN
    angles = (-2.0 * math.pi / CHIP_LEN) * product
    scaling = 1.0 / math.sqrt(CHIP_LEN)
    four_re = np.cos(angles) * scaling
    four_im = np.sin(angles) * scaling
    lag_steps = np.arange(LAG_COUNT) - LAG_COUNT // 2
    frequency = np.where(indices < CHIP_LEN // 2, indices, indices - CHIP_LEN)
    phase_turns = lag_steps[:, None] * frequency[None, :] % (OVERSAMPLE * CHIP_LEN)
    lifted = 2.0 * math.pi / (OVERSAMPLE * CHIP_LEN) * phase_turns
    lift_re = np.cos(lifted) * scaling
    lift_im = np.sin(lifted) * scaling
    lag_values = (lag_steps / OVERSAMPLE).astype(np.float32)

    def left(re, im):
        return np.block([[re, -im], [im, re]])

    def right(re, im):
        pad = ((0, CHIP_LEN - re.shape[0]), (0, 0))
        re2 = np.kron(np.eye(2), np.pad(re, pad).T)
        im2 = np.kron(np.eye(2), np.pad(im, pad).T)
        return np.block([[re2, im2], [-im2, re2]])

    def held(table):
        return jnp.asarray(table.astype(np.float32)).astype(jnp.bfloat16)

    return (
        held(left(four_re, four_im)),
        held(right(four_re, four_im)),
        held(right(lift_re, lift_im)),
        held(left(lift_re, lift_im)),
        lag_values,
    )


def dot(a, b):
    return jnp.dot(a, b, preferred_element_type=jnp.float32)


def gather_kernel(pick_ref, rows_ref, out_ref):
    lines = rows_ref.shape[1]
    rows = jnp.concatenate([rows_ref[0], rows_ref[1]], axis=0)
    out_ref[...] = dot(pick_ref[...], rows).astype(jnp.bfloat16)


def gather_rows(pick, rows):
    width = 1024
    while rows.shape[2] % width:
        width //= 2
    return pl.pallas_call(
        gather_kernel,
        grid=(rows.shape[2] // width,),
        in_specs=[
            pl.BlockSpec(pick.shape, lambda i: (0, 0)),
            pl.BlockSpec((2, rows.shape[1], width), lambda i: (0, 0, i)),
        ],
        out_specs=pl.BlockSpec((pick.shape[0], width), lambda i: (0, i)),
        out_shape=jax.ShapeDtypeStruct((pick.shape[0], rows.shape[2]), jnp.bfloat16),
        name="gather_rows",
    )(pick, rows)


def band_kernel(rel_ref, taps_ref, out_ref):
    blocks = out_ref.shape[0]
    place = lax.broadcasted_iota(jnp.int32, (2 * LANES, LANES), 0)
    for b in range(blocks):
        cols = pl.ds(b * LANES, LANES)
        delta = place - rel_ref[0:1, cols]
        taps = taps_ref[:, cols].astype(jnp.float32)
        band = jnp.zeros((2 * LANES, LANES), jnp.float32)
        for t in range(TAP_COUNT):
            band = jnp.where(delta == t, taps[t : t + 1], band)
        out_ref[b] = band.astype(jnp.bfloat16)


def build_bands(rel, taps):
    count = rel.shape[1] // LANES
    step = 8
    return pl.pallas_call(
        band_kernel,
        grid=(count // step,),
        in_specs=[
            pl.BlockSpec((1, step * LANES), lambda i: (0, i)),
            pl.BlockSpec((TAP_COUNT, step * LANES), lambda i: (0, i)),
        ],
        out_specs=pl.BlockSpec((step, 2 * LANES, LANES), lambda i: (i, 0, 0)),
        out_shape=jax.ShapeDtypeStruct((count, 2 * LANES, LANES), jnp.bfloat16),
        cost_estimate=pl.CostEstimate(
            flops=count * 2 * LANES * LANES * 32, bytes_accessed=count * 65536, transcendentals=0
        ),
        name="build_bands",
    )(rel, taps)


def estimate_kernel(
    off_ref, ref_ref, ref_left, ref_right, sec_ref, sec_top, sec_low, sec_left, sec_right,
    four_ref, spec_ref, lift_ref, corr_ref, lag_ref, out_ref, ref_win, sec_win,
):
    lines = sec_ref.shape[1]
    cols = sec_ref.shape[2]
    chips = cols // SPACING
    rim = (CHIP_LEN - SPACING) // 2
    first = lines // 2 - CHIP_LEN // 2
    f32 = jnp.float32
    blocks = cols // LANES
    high = MARGIN + lines
    for c in range(2):
        for b in range(blocks):
            at = slice(b * LANES, (b + 1) * LANES)
            ref_win[c, b + 1] = ref_ref[c, first : first + CHIP_LEN, at].astype(f32)
            sec_win[c, b + 1, :MARGIN] = sec_top[c, :, at].astype(f32)
            sec_win[c, b + 1, MARGIN:high] = sec_ref[c, :, at].astype(f32)
            sec_win[c, b + 1, high:] = sec_low[c, :, at].astype(f32)
        ref_win[c, 0, :, LANES - rim :] = ref_left[c].astype(f32)
        ref_win[c, blocks + 1, :, :rim] = ref_right[c].astype(f32)
        sec_win[c, 0, :, LANES - MARGIN :] = sec_left[c].astype(f32)
        sec_win[c, blocks + 1, :, :MARGIN] = sec_right[c].astype(f32)
    lane = lax.broadcasted_iota(jnp.int32, (CHIP_LEN, LANES), 1)

    def placed(win, c, row, col, half):
        block = col // LANES
        inner = col - block * LANES
        near = win[c, block, pl.ds(row, CHIP_LEN), :]
        far = win[c, block + 1, pl.ds(row, CHIP_LEN), :]
        turn = (half * CHIP_LEN - inner + LANES) % LANES
        near = pltpu.roll(near, turn, 1)
        far = pltpu.roll(far, turn, 1)
        return jnp.where(lane - half * CHIP_LEN + inner < LANES, near, far)

    def pair(win, rows, cols_at):
        parts = []
        for c in range(2):
            even = placed(win, c, rows[0], cols_at[0], 0)
            odd = placed(win, c, rows[1], cols_at[1], 1)
            parts.append(jnp.where(lane < CHIP_LEN, even, odd).astype(jnp.bfloat16))
        return jnp.concatenate(parts, axis=0)

    def step(i, carry):
        ref_chips, sec_chips = [], []
        for j in range(GROUP):
            g = (i * GROUP + j) * 2
            at = [LANES + SPACING * (g + h) - rim for h in range(2)]
            ref_chips.append(pair(ref_win, (0, 0), at))
            rows = [MARGIN + first + off_ref[0, g + h] for h in range(2)]
            sec_chips.append(pair(sec_win, rows, [at[h] + off_ref[1, g + h] for h in range(2)]))
        both = jnp.concatenate(ref_chips + sec_chips, axis=1)
        half = dot(four_ref[...], both).astype(jnp.bfloat16)
        lhs = jnp.concatenate(
            [
                jnp.concatenate(
                    [
                        half[:CHIP_LEN, j * LANES : (j + 1) * LANES],
                        half[CHIP_LEN:, j * LANES : (j + 1) * LANES],
                    ],
                    axis=1,
                )
                for j in range(2 * GROUP)
            ],
            axis=0,
        )
        spec = dot(lhs, spec_ref[...])
        rows = GROUP * CHIP_LEN
        rr, ri = spec[:rows, :LANES], spec[:rows, LANES:]
        sr, si = spec[rows:, :LANES], spec[rows:, LANES:]
        cross = jnp.concatenate([rr * sr + ri * si, ri * sr - rr * si], axis=1)
        mid = dot(cross.astype(jnp.bfloat16), lift_ref[...]).astype(jnp.bfloat16)
        tall = jnp.concatenate(
            [
                jnp.concatenate(
                    [
                        mid[j * CHIP_LEN : (j + 1) * CHIP_LEN, :LANES],
                        mid[j * CHIP_LEN : (j + 1) * CHIP_LEN, LANES:],
                    ],
                    axis=0,
                )
                for j in range(GROUP)
            ],
            axis=1,
        )
        corr = dot(corr_ref[...], tall)
        energy = corr[:LAG_COUNT] * corr[:LAG_COUNT] + corr[LAG_COUNT:] * corr[LAG_COUNT:]
        weight = energy * energy
        plain = jnp.sum(weight, axis=0, keepdims=True)
        lagged = jnp.sum(weight * lag_ref[...], axis=0, keepdims=True)
        out_ref[i] = jnp.concatenate([plain, lagged], axis=0)
        return carry

    lax.fori_loop(0, chips // (2 * GROUP), step, 0)


def estimate_sums(offsets, ref, ref_sides, sec, sec_rows, sec_sides, tables):
    four, spec, lift, corr, lags = tables
    cols = sec.shape[2]
    lines = sec.shape[1]
    chips = cols // SPACING
    steps = chips // (2 * GROUP)
    vmem = pl.BlockSpec(memory_space=pltpu.VMEM)
    blocks = cols // LANES + 3
    return pl.pallas_call(
        estimate_kernel,
        in_specs=[pl.BlockSpec(memory_space=pltpu.SMEM)] + [vmem] * 13,
        out_specs=vmem,
        out_shape=jax.ShapeDtypeStruct((steps, 2, GROUP * LANES), jnp.float32),
        scratch_shapes=[
            pltpu.VMEM((2, blocks, CHIP_LEN, LANES), jnp.float32),
            pltpu.VMEM((2, blocks, lines + 2 * MARGIN, LANES), jnp.float32),
        ],
        compiler_params=pltpu.CompilerParams(vmem_limit_bytes=VMEM_LIMIT),
        cost_estimate=pl.CostEstimate(
            flops=20_000_000_000, bytes_accessed=8_000_000, transcendentals=0
        ),
        name="estimate_sums",
    )(offsets, ref, *ref_sides, sec, *sec_rows, *sec_sides, four, spec, lift, corr,
      jnp.asarray(lags)[:, None])


def finish_kernel(pick_ref, rows_ref, band_ref, turn_ref, out_ref, wide):
    owned = out_ref.shape[1]
    piece = rows_ref.shape[1]
    count = wide.shape[1] // piece
    total = count * piece
    at = pl.program_id(0)

    @pl.when(at == 0)
    def _():
        wide[:, :MARGIN] = jnp.zeros((2 * owned, MARGIN), jnp.bfloat16)
        wide[:, MARGIN + total : 2 * MARGIN + total] = jnp.zeros((2 * owned, MARGIN), jnp.bfloat16)
        for r in range(count):
            lines = dot(pick_ref[pl.ds(r * 2 * owned, 2 * owned), :], rows_ref[...])
            wide[:, MARGIN + r * piece : MARGIN + (r + 1) * piece] = lines.astype(jnp.bfloat16)

    spread = 2 * LANES // SPACING
    lane = lax.broadcasted_iota(jnp.int32, (2 * spread, 2 * LANES), 1) // SPACING
    chip = lax.broadcasted_iota(jnp.int32, (2 * spread, 2 * LANES), 0) % spread
    expand = (lane == chip).astype(jnp.bfloat16)
    first = at * piece
    for b in range(piece // (2 * LANES)):
        turn = dot(turn_ref[0, b], expand)
        for h in range(2):
            k = 2 * b + h
            window = wide[:, pl.ds(pl.multiple_of(first + k * LANES, LANES), 2 * LANES)]
            s = dot(window, band_ref[k])
            cosine = turn[:owned, h * LANES : (h + 1) * LANES]
            sine = turn[owned:, h * LANES : (h + 1) * LANES]
            s_re, s_im = s[:owned], s[owned:]
            out_ref[0, :, k * LANES : (k + 1) * LANES] = (s_re * cosine + s_im * sine).astype(
                jnp.bfloat16
            )
            out_ref[1, :, k * LANES : (k + 1) * LANES] = (s_im * cosine - s_re * sine).astype(
                jnp.bfloat16
            )


def finish(pick, rows, bands, turns, owner_cap):
    piece = rows.shape[1]
    count = turns.shape[0]
    blocks = piece // LANES
    return pl.pallas_call(
        finish_kernel,
        grid=(count,),
        in_specs=[
            pl.BlockSpec(pick.shape, lambda i: (0, 0)),
            pl.BlockSpec(rows.shape, lambda i: (0, 0)),
            pl.BlockSpec((blocks, 2 * LANES, LANES), lambda i: (i, 0, 0)),
            pl.BlockSpec((1,) + turns.shape[1:], lambda i: (i, 0, 0, 0)),
        ],
        out_specs=pl.BlockSpec((2, owner_cap, piece), lambda i: (0, 0, i)),
        out_shape=jax.ShapeDtypeStruct((2, owner_cap, count * piece), jnp.bfloat16),
        scratch_shapes=[pltpu.VMEM((2 * owner_cap, count * piece + 2 * MARGIN), jnp.bfloat16)],
        compiler_params=pltpu.CompilerParams(vmem_limit_bytes=VMEM_LIMIT),
        name="finish_lines",
    )(pick, rows, bands, turns)


def per_device(
    reference_slc, secondary_slc, chip_offsets, src_row, line_owner, band_start, band_taps
):
    tables = make_tables()
    lines_dev = secondary_slc.shape[1]
    cols_dev = secondary_slc.shape[2]
    chip_count = cols_dev // SPACING
    az_count = lax.axis_size("az")
    rg_count = lax.axis_size("rg")
    owners = az_count * rg_count
    pair_cap = max(2, (lines_dev + 2 * MAX_SHIFT + owners - 1) // owners)
    owner_cap = pair_cap * az_count
    total_cols = cols_dev * rg_count
    rim = (CHIP_LEN - SPACING) // 2
    first_row = lines_dev // 2 - CHIP_LEN // 2
    az_index = lax.axis_index("az")
    rg_index = lax.axis_index("rg")
    me_owner = az_index * rg_count + rg_index

    count = src_row.shape[0]
    ids = jnp.arange(count, dtype=jnp.int32)
    src_tile = src_row // lines_dev
    mine = (line_owner[:, None] == line_owner[None, :]) & (ids[:, None] < ids[None, :])
    own_rank = jnp.sum(mine.astype(jnp.int32), axis=0)
    near = mine & (src_tile[:, None] == src_tile[None, :])
    pair_rank = jnp.sum(near.astype(jnp.int32), axis=0)

    local_row = src_row - az_index * lines_dev
    slot = jnp.where(src_tile == az_index, line_owner * pair_cap + pair_rank, -1)
    slots = jnp.arange(owners * pair_cap, dtype=jnp.int32)
    send_row = jnp.sum(
        jnp.where(slots[:, None] == slot[None, :], local_row[None, :] + 1, 0), axis=1
    ) - 1
    send_row = send_row.reshape(owners, 1, pair_cap)
    part = jnp.arange(2, dtype=jnp.int32)[None, :, None] * lines_dev
    target = jnp.where(send_row >= 0, send_row + part, -1).reshape(-1)
    send_pick = (
        target[:, None] == jnp.arange(2 * lines_dev, dtype=jnp.int32)[None, :]
    ).astype(jnp.bfloat16)
    outgoing = gather_rows(send_pick, secondary_slc)
    arrived = lax.all_to_all(outgoing, ("az", "rg"), split_axis=0, concat_axis=0, tiled=True)

    ref_rows = reference_slc[:, first_row : first_row + CHIP_LEN, :]
    ref_sides = (
        shifted(ref_rows[:, :, cols_dev - rim :], "rg", True),
        shifted(ref_rows[:, :, :rim], "rg", False),
    )
    sec_rows = (
        shifted(secondary_slc[:, lines_dev - MARGIN :, :], "az", True),
        shifted(secondary_slc[:, :MARGIN, :], "az", False),
    )
    tall_right = jnp.concatenate(
        [a[:, :, cols_dev - MARGIN :] for a in (sec_rows[0], secondary_slc, sec_rows[1])], axis=1
    )
    tall_left = jnp.concatenate(
        [a[:, :, :MARGIN] for a in (sec_rows[0], secondary_slc, sec_rows[1])], axis=1
    )
    sec_sides = (shifted(tall_right, "rg", True), shifted(tall_left, "rg", False))

    offsets = chip_offsets[:, 0]
    sums = estimate_sums(
        offsets, reference_slc, ref_sides, secondary_slc, sec_rows, sec_sides, tables
    )
    sums = jnp.moveaxis(sums, 1, 0).reshape(2, chip_count, CHIP_LEN)
    lag_wide = jnp.asarray(np.pad(tables[4], (0, CHIP_LEN - LAG_COUNT)))
    totals = jnp.sum(sums[0], axis=1) + EPS
    cent_az = jnp.sum(sums[1], axis=1) / totals
    cent_rg = jnp.sum(sums[0] * lag_wide[None, :], axis=1) / totals
    est = jnp.stack([cent_az, cent_rg]) + offsets.astype(jnp.float32)
    everywhere = lax.all_to_all(
        jnp.broadcast_to(est[0][None], (owners, chip_count)),
        ("az", "rg"),
        split_axis=0,
        concat_axis=0,
        tiled=True,
    ).reshape(az_count, rg_count, chip_count)

    all_cols = jnp.arange(total_cols, dtype=jnp.int32)
    rel = (band_start - all_cols // LANES * LANES + MARGIN)[None, :]
    bands = build_bands(rel, band_taps)

    outs = jnp.arange(owner_cap, dtype=jnp.int32)
    placed = (own_rank[None, :] == outs[:, None]) & (line_owner == me_owner)[None, :]
    which = jnp.sum(
        jnp.where(placed, (src_tile * pair_cap + pair_rank + 1)[None, :], 0), axis=1
    ) - 1
    tile = which // pair_cap
    from_rank = which % pair_cap
    rg_ids = jnp.arange(rg_count, dtype=jnp.int32)[:, None, None]
    parts = jnp.arange(2, dtype=jnp.int32)[None, :, None]
    source = ((tile[None, None] * rg_count + rg_ids) * 2 + parts) * pair_cap + from_rank[None, None]
    source = jnp.where(which[None, None] >= 0, source, -1).reshape(-1)
    recv_pick = (
        source[:, None] == jnp.arange(owners * 2 * pair_cap, dtype=jnp.int32)[None, :]
    ).astype(jnp.bfloat16)

    tiles = jnp.arange(az_count, dtype=jnp.int32)
    chosen = jnp.sum(
        jnp.where(
            (tile[:, None] == tiles[None, :])[:, :, None, None], everywhere[None], 0.0
        ),
        axis=1,
    )
    angle = PHASE_RATE * chosen
    spread = 2 * LANES // SPACING
    turns = jnp.stack([jnp.cos(angle), jnp.sin(angle)])
    high = turns.astype(jnp.bfloat16)
    low = (turns - high.astype(jnp.float32)).astype(jnp.bfloat16)
    turns = jnp.stack([high, low], axis=0).reshape(
        2, 2, owner_cap, rg_count, chip_count // spread, spread
    )
    turns = turns.transpose(3, 4, 1, 2, 0, 5).reshape(
        rg_count, chip_count // spread, 2 * owner_cap, 2 * spread
    )
    lines_out = finish(recv_pick, arrived, bands, turns, owner_cap)
    return (est[:, None, :], lines_out)


def solution(mesh):
    return jax.shard_map(
        per_device,
        mesh=mesh,
        in_specs=(
            P(None, "az", "rg"),
            P(None, "az", "rg"),
            P(None, "az", "rg"),
            P(),
            P(),
            P(),
            P(),
        ),
        out_specs=(P(None, "az", "rg"), P(None, ("az", "rg"), None)),
        check_vma=False,
    )
```

profile of v0, /device:TPU:1, one launch (start us, length us, event | category | flops | bytes accessed | tf_op | source)
XLA Modules:
  0.0 114.7 jit_solution(2100022157944428249)
XLA Ops:
  0.6 0.0 copy-start.3
  0.6 0.0 copy-start.1
  0.6 0.9 fusion.17
  1.5 1.3 %collective-permute-start.1 = (bf16[2,64,16]{2,1,0:T(8,128)(2,1)S(1)}, bf16[2,64,16]{2,1,0:T(8,128)(2,1)S(1)}, u32[]{:S(2)}, u32[]{:S(2)}) collective-permute-start(bf16[2,64,16]{2,1,0:T(8,128)(2,1)S(1)} %get-tuple-element.15), channel_id=1, source_target_pairs={{1,0},{2,1},{3,2},{5,4},{6,5},{7,6},{9,8},{10,9},{11,10},{13,12},{... | collective-permute-start | bytes 12296 | tf_op jit(solution)/shard_map/ppermute | solution.py:33
  2.8 4.6 %collective-permute-start = (bf16[2,64,16]{2,1,0:T(8,128)(2,1)S(1)}, bf16[2,64,16]{2,1,0:T(8,128)(2,1)S(1)}, u32[]{:S(2)}, u32[]{:S(2)}) collective-permute-start(bf16[2,64,16]{2,1,0:T(8,128)(2,1)S(1)} %get-tuple-element.16), channel_id=1, source_target_pairs={{0,1},{1,2},{2,3},{4,5},{5,6},{6,7},{8,9},{9,10},{10,11},{12,13},{... | collective-permute-start | bytes 12296 | tf_op jit(solution)/shard_map/ppermute | solution.py:33
  7.5 1.5 %fusion.16 = (bf16[2,64,3072]{2,1,0:T(8,128)(2,1)S(1)}, bf16[2,64,3072]{2,1,0:T(8,128)(2,1)S(1)}) fusion(bf16[2,96,3072]{2,1,0:T(8,128)(2,1)} %rows_ref.1), kind=kLoop, calls=%fused_computation.66 | loop fusion | bytes 3145728 | tf_op jit(solution)/shard_map/slice | solution.py:360
  9.0 2.9 %collective-permute-start.3 = (bf16[2,64,3072]{2,1,0:T(8,128)(2,1)S(1)}, bf16[2,64,3072]{2,1,0:T(8,128)(2,1)S(1)}, u32[]{:S(2)}, u32[]{:S(2)}) collective-permute-start(bf16[2,64,3072]{2,1,0:T(8,128)(2,1)S(1)} %get-tuple-element.13), channel_id=1, source_target_pairs={{4,0},{8,4},{12,8},{16,12},{20,16},{24,20},{28,24},{5,1},{9,5},{13... | collective-permute-start | bytes 2359304 | tf_op jit(solution)/shard_map/ppermute | solution.py:33
  11.8 3.5 %collective-permute-start.2 = (bf16[2,64,3072]{2,1,0:T(8,128)(2,1)S(1)}, bf16[2,64,3072]{2,1,0:T(8,128)(2,1)S(1)}, u32[]{:S(2)}, u32[]{:S(2)}) collective-permute-start(bf16[2,64,3072]{2,1,0:T(8,128)(2,1)S(1)} %get-tuple-element.14), channel_id=1, source_target_pairs={{0,4},{4,8},{8,12},{12,16},{16,20},{20,24},{24,28},{1,5},{5,9},{9,... | collective-permute-start | bytes 2359304 | tf_op jit(solution)/shard_map/ppermute | solution.py:33
  15.3 0.0 copy-done.3
  15.3 0.0 copy-done.1
  15.3 0.5 convert_reduce_fusion.1
  15.8 0.1 select_reduce_fusion.1
  16.0 0.1 sub.54
  16.1 0.1 add_select_fusion.1
  16.2 0.1 select_n.81
  16.3 0.9 fusion.15
  17.2 11.1 %collective-permute-done.3.sec_low = bf16[2,64,3072]{2,1,0:T(8,128)(2,1)S(1)} collective-permute-done((bf16[2,64,3072]{2,1,0:T(8,128)(2,1)S(1)}, bf16[2,64,3072]{2,1,0:T(8,128)(2,1)S(1)}, u32[]{:S(2)}, u32[]{:S(2)}) %collective-permute-start.3) | collective-permute-done | bytes 786464 | tf_op jit(solution)/shard_map/ppermute | solution.py:33
  28.3 0.1 fusion.19
  28.4 0.0 collective-permute-done.2.sec_top
  28.4 0.0 copy-start.5
  28.4 0.1 fusion.18
  28.5 3.2 %collective-permute-start.4 = (bf16[2,224,64]{2,1,0:T(8,128)(2,1)S(1)}, bf16[2,224,64]{2,1,0:T(8,128)(2,1)S(1)}, u32[]{:S(2)}, u32[]{:S(2)}) collective-permute-start(bf16[2,224,64]{2,1,0:T(8,128)(2,1)S(1)} %pad_maximum_fusion.1), channel_id=1, source_target_pairs={{0,1},{1,2},{2,3},{4,5},{5,6},{6,7},{8,9},{9,10},{10,11},{12,13},{... | collective-permute-start | bytes 172040 | tf_op jit(solution)/shard_map/ppermute | solution.py:33
  31.8 1.3 %collective-permute-start.5 = (bf16[2,224,64]{2,1,0:T(8,128)(2,1)S(1)}, bf16[2,224,64]{2,1,0:T(8,128)(2,1)S(1)}, u32[]{:S(2)}, u32[]{:S(2)}) collective-permute-start(bf16[2,224,64]{2,1,0:T(8,128)(2,1)S(1)} %pad_maximum_fusion.2), channel_id=1, source_target_pairs={{1,0},{2,1},{3,2},{5,4},{6,5},{7,6},{9,8},{10,9},{11,10},{13,12},{... | collective-permute-start | bytes 172040 | tf_op jit(solution)/shard_map/ppermute | solution.py:33
  33.1 0.8 fusion.3.pick_ref
  33.8 0.0 collective-permute-done.1.ref_right
  33.8 0.0 collective-permute-done.ref_left
  33.8 0.0 copy-start.11
  33.9 0.0 collective-permute-done.4.sec_left
  33.9 3.4 %collective-permute-done.5.sec_right = bf16[2,224,64]{2,1,0:T(8,128)(2,1)S(1)} collective-permute-done((bf16[2,224,64]{2,1,0:T(8,128)(2,1)S(1)}, bf16[2,224,64]{2,1,0:T(8,128)(2,1)S(1)}, u32[]{:S(2)}, u32[]{:S(2)}) %collective-permute-start.5) | collective-permute-done | bytes 57376 | tf_op jit(solution)/shard_map/ppermute | solution.py:33
  37.3 0.0 copy-done.5
  37.3 0.0 copy-done.11
  37.3 0.0 copy-done.8
  37.4 0.6 copy-done.9
  38.0 10.9 %estimate_sums.1 = f32[6,2,1024]{2,1,0:T(2,128)} custom-call(s32[2,96]{1,0:T(2,128)} %bitcast.31, bf16[2,96,3072]{2,1,0:T(8,128)(2,1)} %ref_ref.1, bf16[2,64,16]{2,1,0:T(8,128)(2,1)} %copy-done.11, bf16[2,64,16]{2,1,0:T(8,128)(2,1)} %copy-done.10, bf16[2,96,3072]{2,1,0:T(8,128)(2,1)} %rows_ref.1, bf16[2,64,3072]{2,1,0:T(8,128)(2,1)} %copy-done.5, ...), custom_call_target="tpu_custom_call" | custom-call | flops 20000000000 | bytes 8000000 | tf_op jit(solution)/shard_map/estimate_sums/pallas_call | solution.py:235
  48.9 1.0 slice_reduce_fusion.1
  49.9 0.1 squeeze.11
  49.9 0.1 squeeze.12
  50.0 0.1 reduce_sum.72
  50.1 0.1 fusion.14
  50.3 0.0 copy-done.6
  50.3 0.6 broadcast_in_dim.120
  50.9 8.1 %all-to-all-start.1 = ((f32[32,1,96]{2,1,0:T(1,128)}), f32[32,1,96]{2,1,0:T(1,128)S(1)}, u32[]{:S(2)}, u32[]{:S(2)}) async-start(f32[32,1,96]{2,1,0:T(1,128)} %broadcast_in_dim.120), calls=%async_computation.1 | async-start | bytes 32768 | tf_op jit(solution)/shard_map/all_to_all | solution.py:380
  59.0 0.0 copy-start.2
  59.0 3.6 %gather_rows.1 = bf16[256,3072]{1,0:T(8,128)(2,1)} custom-call(bf16[256,192]{1,0:T(8,128)(2,1)} %fusion.3.pick_ref, bf16[2,96,3072]{2,1,0:T(8,128)(2,1)} %rows_ref.1), custom_call_target="tpu_custom_call" | custom-call | tf_op jit(solution)/shard_map/gather_rows/pallas_call | solution.py:86
  62.6 3.1 %all-to-all-done.1 = f32[32,1,96]{2,1,0:T(1,128)S(1)} async-done(((f32[32,1,96]{2,1,0:T(1,128)}), f32[32,1,96]{2,1,0:T(1,128)S(1)}, u32[]{:S(2)}, u32[]{:S(2)}) %all-to-all-start.1) | async-done | bytes 12320 | tf_op jit(solution)/shard_map/all_to_all | solution.py:380
  65.7 3.0 %all-to-all-start = ((bf16[32,8,3072]{2,1,0:T(8,128)(2,1)}), bf16[32,8,3072]{2,1,0:T(8,128)(2,1)S(1)}, u32[]{:S(2)}, u32[]{:S(2)}) async-start(bf16[32,8,3072]{2,1,0:T(8,128)(2,1)} %bitcast.19), calls=%async_computation | async-start | bytes 3145728 | tf_op jit(solution)/shard_map/all_to_all | solution.py:351
  68.7 0.1 select_reduce_fusion.2
  68.9 0.1 select_n.77
  69.0 0.6 fusion.9
  69.6 10.1 %build_bands.1.band_ref = bf16[96,256,128]{2,1,0:T(8,128)(2,1)} custom-call(s32[1,12288]{1,0:T(1,128)} %bitcast.24, bf16[8,12288]{1,0:T(8,128)(2,1)} %taps_ref.1), custom_call_target="tpu_custom_call" | custom-call | flops 100663296 | bytes 6291456 | tf_op jit(solution)/shard_map/build_bands/pallas_call | solution.py:115
  79.8 0.1 iota_compare_fusion.5
  79.8 0.8 fusion.2.pick_ref
  80.6 0.6 maximum_add_fusion
  81.2 0.3 select_reduce_fusion
  81.4 0.2 fusion.6
  81.7 0.1 copy.26
  81.8 0.1 copy.27
  82.0 0.1 maximum_bitcast_fusion
  82.1 0.5 copy.28
  82.7 0.2 reshape.366
  82.9 1.3 %copy.29.turn_ref = bf16[4,12,64,16]{3,2,1,0:T(8,128)(2,1)} copy(bf16[4,12,64,16]{2,3,1,0:T(8,128)(2,1)S(1)} %reshape.366) | data formatting | bytes 196608 | tf_op jit(solution)/shard_map/reshape | solution.py:422
  84.1 22.1 %all-to-all-done = bf16[32,8,3072]{2,1,0:T(8,128)(2,1)S(1)} async-done(((bf16[32,8,3072]{2,1,0:T(8,128)(2,1)}), bf16[32,8,3072]{2,1,0:T(8,128)(2,1)S(1)}, u32[]{:S(2)}, u32[]{:S(2)}) %all-to-all-start) | async-done | bytes 1572896 | tf_op jit(solution)/shard_map/all_to_all | solution.py:351
  106.3 1.1 copy-done
  107.4 7.3 %finish_lines.1 = bf16[2,32,12288]{2,1,0:T(8,128)(2,1)} custom-call(bf16[256,256]{1,0:T(8,128)(2,1)} %fusion.2.pick_ref, bf16[256,3072]{1,0:T(8,128)(2,1)} %bitcast.18, bf16[96,256,128]{2,1,0:T(8,128)(2,1)} %build_bands.1.band_ref, bf16[4,12,64,16]{3,2,1,0:T(8,128)(2,1)} %copy.29.turn_ref), custom_call_target="tpu_custom_call" | custom-call | tf_op jit(solution)/shard_map/finish_lines/pallas_call | solution.py:294
  (30 shorter events, 0.3 us)
Async XLA Ops:
  0.6 14.7 %copy-start.3 = (s32[768]{0:T(1024)S(1)}, s32[768]{0:T(1024)}, u32[]{:S(2)}) copy-start(s32[768]{0:T(1024)} %param.16) | copy-start | bytes 9220
  0.6 14.7 %copy-start.1 = (s32[768]{0:T(1024)S(1)}, s32[768]{0:T(1024)}, u32[]{:S(2)}) copy-start(s32[768]{0:T(1024)} %param.17) | copy-start | bytes 9220
  1.5 32.3 %collective-permute-start.1 = (bf16[2,64,16]{2,1,0:T(8,128)(2,1)S(1)}, bf16[2,64,16]{2,1,0:T(8,128)(2,1)S(1)}, u32[]{:S(2)}, u32[]{:S(2)}) collective-permute-start(bf16[2,64,16]{2,1,0:T(8,128)(2,1)S(1)} %get-tuple-element.15), channel_id=1, source_target_pairs={{1,0},{2,1},{3,2},{5,4},{6,5},{7,6},{9,8},{10,9},{11,10},{13,12},{... | collective-permute-start | bytes 12296 | tf_op jit(solution)/shard_map/ppermute | solution.py:33
  2.8 31.0 %collective-permute-start = (bf16[2,64,16]{2,1,0:T(8,128)(2,1)S(1)}, bf16[2,64,16]{2,1,0:T(8,128)(2,1)S(1)}, u32[]{:S(2)}, u32[]{:S(2)}) collective-permute-start(bf16[2,64,16]{2,1,0:T(8,128)(2,1)S(1)} %get-tuple-element.16), channel_id=1, source_target_pairs={{0,1},{1,2},{2,3},{4,5},{5,6},{6,7},{8,9},{9,10},{10,11},{12,13},{... | collective-permute-start | bytes 12296 | tf_op jit(solution)/shard_map/ppermute | solution.py:33
  9.0 19.4 %collective-permute-start.3 = (bf16[2,64,3072]{2,1,0:T(8,128)(2,1)S(1)}, bf16[2,64,3072]{2,1,0:T(8,128)(2,1)S(1)}, u32[]{:S(2)}, u32[]{:S(2)}) collective-permute-start(bf16[2,64,3072]{2,1,0:T(8,128)(2,1)S(1)} %get-tuple-element.13), channel_id=1, source_target_pairs={{4,0},{8,4},{12,8},{16,12},{20,16},{24,20},{28,24},{5,1},{9,5},{13... | collective-permute-start | bytes 2359304 | tf_op jit(solution)/shard_map/ppermute | solution.py:33
  11.8 16.6 %collective-permute-start.2 = (bf16[2,64,3072]{2,1,0:T(8,128)(2,1)S(1)}, bf16[2,64,3072]{2,1,0:T(8,128)(2,1)S(1)}, u32[]{:S(2)}, u32[]{:S(2)}) collective-permute-start(bf16[2,64,3072]{2,1,0:T(8,128)(2,1)S(1)} %get-tuple-element.14), channel_id=1, source_target_pairs={{0,4},{4,8},{8,12},{12,16},{16,20},{20,24},{24,28},{1,5},{5,9},{9,... | collective-permute-start | bytes 2359304 | tf_op jit(solution)/shard_map/ppermute | solution.py:33
  28.3 9.0 %copy-start.4 = (bf16[2,64,3072]{2,1,0:T(8,128)(2,1)}, bf16[2,64,3072]{2,1,0:T(8,128)(2,1)S(1)}, u32[]{:S(2)}) copy-start(bf16[2,64,3072]{2,1,0:T(8,128)(2,1)S(1)} %collective-permute-done.3.sec_low) | copy-start | bytes 2359300
  28.4 8.9 %copy-start.5 = (bf16[2,64,3072]{2,1,0:T(8,128)(2,1)}, bf16[2,64,3072]{2,1,0:T(8,128)(2,1)S(1)}, u32[]{:S(2)}) copy-start(bf16[2,64,3072]{2,1,0:T(8,128)(2,1)S(1)} %collective-permute-done.2.sec_top) | copy-start | bytes 2359300
  28.5 5.3 %collective-permute-start.4 = (bf16[2,224,64]{2,1,0:T(8,128)(2,1)S(1)}, bf16[2,224,64]{2,1,0:T(8,128)(2,1)S(1)}, u32[]{:S(2)}, u32[]{:S(2)}) collective-permute-start(bf16[2,224,64]{2,1,0:T(8,128)(2,1)S(1)} %pad_maximum_fusion.1), channel_id=1, source_target_pairs={{0,1},{1,2},{2,3},{4,5},{5,6},{6,7},{8,9},{9,10},{10,11},{12,13},{... | collective-permute-start | bytes 172040 | tf_op jit(solution)/shard_map/ppermute | solution.py:33
  31.8 5.5 %collective-permute-start.5 = (bf16[2,224,64]{2,1,0:T(8,128)(2,1)S(1)}, bf16[2,224,64]{2,1,0:T(8,128)(2,1)S(1)}, u32[]{:S(2)}, u32[]{:S(2)}) collective-permute-start(bf16[2,224,64]{2,1,0:T(8,128)(2,1)S(1)} %pad_maximum_fusion.2), channel_id=1, source_target_pairs={{1,0},{2,1},{3,2},{5,4},{6,5},{7,6},{9,8},{10,9},{11,10},{13,12},{... | collective-permute-start | bytes 172040 | tf_op jit(solution)/shard_map/ppermute | solution.py:33
  33.8 3.5 %copy-start.10 = (bf16[2,64,16]{2,1,0:T(8,128)(2,1)}, bf16[2,64,16]{2,1,0:T(8,128)(2,1)S(1)}, u32[]{:S(2)}) copy-start(bf16[2,64,16]{2,1,0:T(8,128)(2,1)S(1)} %collective-permute-done.1.ref_right) | copy-start | bytes 12292
  33.8 3.5 %copy-start.11 = (bf16[2,64,16]{2,1,0:T(8,128)(2,1)}, bf16[2,64,16]{2,1,0:T(8,128)(2,1)S(1)}, u32[]{:S(2)}) copy-start(bf16[2,64,16]{2,1,0:T(8,128)(2,1)S(1)} %collective-permute-done.ref_left) | copy-start | bytes 12292
  33.9 3.5 %copy-start.8 = (bf16[2,224,64]{2,1,0:T(8,128)(2,1)}, bf16[2,224,64]{2,1,0:T(8,128)(2,1)S(1)}, u32[]{:S(2)}) copy-start(bf16[2,224,64]{2,1,0:T(8,128)(2,1)S(1)} %collective-permute-done.4.sec_left) | copy-start | bytes 172036
  37.3 0.6 copy-start.9
  38.0 12.2 %copy-start.7 = (f32[64]{0:T(128)S(1)}, f32[64]{0:T(128)}, u32[]{:S(2)}) copy-start(f32[64]{0:T(128)} %constant.102.clone) | copy-start | bytes 772
  38.0 12.3 %copy-start.6 = (s32[2,1,96]{2,1,0:T(1,128)S(1)}, s32[2,1,96]{2,1,0:T(1,128)}, u32[]{:S(2)}) copy-start(s32[2,1,96]{2,1,0:T(1,128)} %param.15) | copy-start | bytes 2308
  50.9 14.8 %all-to-all-start.1 = ((f32[32,1,96]{2,1,0:T(1,128)}), f32[32,1,96]{2,1,0:T(1,128)S(1)}, u32[]{:S(2)}, u32[]{:S(2)}) async-start(f32[32,1,96]{2,1,0:T(1,128)} %broadcast_in_dim.120), calls=%async_computation.1 | async-start | bytes 32768 | tf_op jit(solution)/shard_map/all_to_all | solution.py:380
  59.0 10.0 %copy-start.2 = (s32[12288]{0:T(1024)S(1)}, s32[12288]{0:T(1024)}, u32[]{:S(2)}) copy-start(s32[12288]{0:T(1024)} %param.18) | copy-start | bytes 147460
  65.7 40.6 %all-to-all-start = ((bf16[32,8,3072]{2,1,0:T(8,128)(2,1)}), bf16[32,8,3072]{2,1,0:T(8,128)(2,1)S(1)}, u32[]{:S(2)}, u32[]{:S(2)}) async-start(bf16[32,8,3072]{2,1,0:T(8,128)(2,1)} %bitcast.19), calls=%async_computation | async-start | bytes 3145728 | tf_op jit(solution)/shard_map/all_to_all | solution.py:351
  106.3 1.1 copy-start
where the time goes:
time: 116 us; the launch traced here: 115 us
  waiting for transfers between devices  39.8 us (34%)
  Pallas kernels  31.9 us (28%)
  starting transfers between devices  27.8 us (24%)
  local copies, waits for them, and re-layouts  9.49 us (8%)
  other arithmetic  4.64 us (4%)
    all_to_all x1, waiting for transfers between devices, per_device(): lax.all_to_all(outgoing, ('az', 'rg'), split_axis=0, concat_axis=0, tiled...  22.1 us
    ppermute x6, starting transfers between devices, shifted(): return lax.ppermute(cells, axis, pairs)  16.8 us
    ppermute x6, waiting for transfers between devices, shifted(): return lax.ppermute(cells, axis, pairs)  14.5 us
    pallas_call x1, Pallas kernels, estimate_sums(): pl.pallas_call(estimate_kernel, in_specs=[pl.BlockSpec(memory_space=pltpu...  10.9 us
    pallas_call x1, Pallas kernels, build_bands(): pl.pallas_call(band_kernel, grid=(count // step,), in_specs=[pl.BlockSpec...  10.1 us
    all_to_all x1, starting transfers between devices, per_device(): lax.all_to_all(jnp.broadcast_to(est[0][None], (owners, chip_count)), ('az...  8.05 us
    pallas_call x1, Pallas kernels, finish(): pl.pallas_call(finish_kernel, grid=(count,), in_specs=[pl.BlockSpec(pick....  7.29 us
    pallas_call x1, Pallas kernels, gather_rows(): pl.pallas_call(gather_kernel, grid=(rows.shape[2] // width,), in_specs=[p...  3.6 us
  transfers between devices with their start and end apart: 8, of which 4 were waited for; matrix products, arithmetic and copies ran while one was open for 8% of the time, Pallas kernels for 12%

commit v1 on v0

--- a/solution.py
+++ b/solution.py
@@ -24,13 +24,16 @@
 VMEM_LIMIT = 56 * 1024 * 1024
 
 
-def shifted(cells, axis, up):
-    count = lax.axis_size(axis)
-    if up:
-        pairs = [(i, i + 1) for i in range(count - 1)]
-    else:
-        pairs = [(i + 1, i) for i in range(count - 1)]
-    return lax.ppermute(cells, axis, pairs)
+def moved(cells, az_step, rg_step):
+    az_count = lax.axis_size("az")
+    rg_count = lax.axis_size("rg")
+    pairs = [
+        (a * rg_count + r, (a + az_step) * rg_count + r + rg_step)
+        for a in range(az_count)
+        for r in range(rg_count)
+        if 0 <= a + az_step < az_count and 0 <= r + rg_step < rg_count
+    ]
+    return lax.ppermute(cells, ("az", "rg"), pairs)
 
 
 def make_tables():
@@ -129,8 +132,9 @@
 
 
 def estimate_kernel(
-    off_ref, ref_ref, ref_left, ref_right, sec_ref, sec_top, sec_low, sec_left, sec_right,
-    four_ref, spec_ref, lift_ref, corr_ref, lag_ref, out_ref, ref_win, sec_win,
+    off_ref, ref_ref, sec_ref, sec_top, sec_low, left, right, top_left, top_right, low_left,
+    low_right, four_ref, spec_ref, lift_ref, corr_ref, lag_ref, wide_ref, out_ref, ref_win,
+    sec_win, plain_ref, lagged_ref,
 ):
     lines = sec_ref.shape[1]
     cols = sec_ref.shape[2]
@@ -147,10 +151,14 @@
             sec_win[c, b + 1, :MARGIN] = sec_top[c, :, at].astype(f32)
             sec_win[c, b + 1, MARGIN:high] = sec_ref[c, :, at].astype(f32)
             sec_win[c, b + 1, high:] = sec_low[c, :, at].astype(f32)
-        ref_win[c, 0, :, LANES - rim :] = ref_left[c].astype(f32)
-        ref_win[c, blocks + 1, :, :rim] = ref_right[c].astype(f32)
-        sec_win[c, 0, :, LANES - MARGIN :] = sec_left[c].astype(f32)
-        sec_win[c, blocks + 1, :, :MARGIN] = sec_right[c].astype(f32)
+        ref_win[c, 0, :, LANES - MARGIN :] = left[c, lines:].astype(f32)
+        ref_win[c, blocks + 1, :, :MARGIN] = right[c, lines:].astype(f32)
+        sec_win[c, 0, :MARGIN, LANES - MARGIN :] = top_left[c].astype(f32)
+        sec_win[c, 0, MARGIN:high, LANES - MARGIN :] = left[c, :lines].astype(f32)
+        sec_win[c, 0, high:, LANES - MARGIN :] = low_left[c].astype(f32)
+        sec_win[c, blocks + 1, :MARGIN, :MARGIN] = top_right[c].astype(f32)
+        sec_win[c, blocks + 1, MARGIN:high, :MARGIN] = right[c, :lines].astype(f32)
+        sec_win[c, blocks + 1, high:, :MARGIN] = low_right[c].astype(f32)
     lane = lax.broadcasted_iota(jnp.int32, (CHIP_LEN, LANES), 1)
 
     def placed(win, c, row, col, half):
@@ -218,42 +226,59 @@
         weight = energy * energy
         plain = jnp.sum(weight, axis=0, keepdims=True)
         lagged = jnp.sum(weight * lag_ref[...], axis=0, keepdims=True)
-        out_ref[i] = jnp.concatenate([plain, lagged], axis=0)
+        for j in range(GROUP):
+            at = slice(j * LANES, (j + 1) * LANES)
+            plain_ref[pl.ds(i * GROUP + j, 1), :] = plain[:, at]
+            lagged_ref[pl.ds(i * GROUP + j, 1), :] = lagged[:, at]
         return carry
 
     lax.fori_loop(0, chips // (2 * GROUP), step, 0)
-
-
-def estimate_sums(offsets, ref, ref_sides, sec, sec_rows, sec_sides, tables):
+    near = lax.broadcasted_iota(jnp.int32, (chips // 2, LANES), 1) < CHIP_LEN
+    plain = plain_ref[...]
+    lagged = lagged_ref[...]
+    across = plain * wide_ref[...]
+    for h in range(2):
+        inside = near if h == 0 else jnp.logical_not(near)
+        total = jnp.sum(jnp.where(inside, plain, 0.0), axis=1, keepdims=True) + EPS
+        out_ref[0, :, h : h + 1] = (
+            jnp.sum(jnp.where(inside, lagged, 0.0), axis=1, keepdims=True) / total
+        )
+        out_ref[1, :, h : h + 1] = (
+            jnp.sum(jnp.where(inside, across, 0.0), axis=1, keepdims=True) / total
+        )
+
+
+def estimate_shifts(offsets, ref, sec, halos, tables):
     four, spec, lift, corr, lags = tables
-    cols = sec.shape[2]
     lines = sec.shape[1]
-    chips = cols // SPACING
-    steps = chips // (2 * GROUP)
+    chips = sec.shape[2] // SPACING
     vmem = pl.BlockSpec(memory_space=pltpu.VMEM)
-    blocks = cols // LANES + 3
+    blocks = sec.shape[2] // LANES + 3
+    lag_wide = np.tile(np.pad(lags, (0, CHIP_LEN - LAG_COUNT)), 2)[None, :]
     return pl.pallas_call(
         estimate_kernel,
-        in_specs=[pl.BlockSpec(memory_space=pltpu.SMEM)] + [vmem] * 13,
+        in_specs=[pl.BlockSpec(memory_space=pltpu.SMEM)] + [vmem] * 16,
         out_specs=vmem,
-        out_shape=jax.ShapeDtypeStruct((steps, 2, GROUP * LANES), jnp.float32),
+        out_shape=jax.ShapeDtypeStruct((2, chips // 2, 2), jnp.float32),
         scratch_shapes=[
             pltpu.VMEM((2, blocks, CHIP_LEN, LANES), jnp.float32),
             pltpu.VMEM((2, blocks, lines + 2 * MARGIN, LANES), jnp.float32),
+            pltpu.VMEM((chips // 2, LANES), jnp.float32),
+            pltpu.VMEM((chips // 2, LANES), jnp.float32),
         ],
         compiler_params=pltpu.CompilerParams(vmem_limit_bytes=VMEM_LIMIT),
         cost_estimate=pl.CostEstimate(
-            flops=20_000_000_000, bytes_accessed=8_000_000, transcendentals=0
+            flops=10_000_000_000, bytes_accessed=8_000_000, transcendentals=0
         ),
-        name="estimate_sums",
-    )(offsets, ref, *ref_sides, sec, *sec_rows, *sec_sides, four, spec, lift, corr,
-      jnp.asarray(lags)[:, None])
-
-
-def finish_kernel(pick_ref, rows_ref, band_ref, turn_ref, out_ref, wide):
+        name="estimate_shifts",
+    )(offsets, ref, sec, *halos, four, spec, lift, corr, jnp.asarray(lags)[:, None],
+      jnp.asarray(lag_wide))
+
+
+def resample_kernel(pick_ref, rows_ref, band_ref, out_ref, wide):
     owned = out_ref.shape[1]
     piece = rows_ref.shape[1]
-    count = wide.shape[1] // piece
+    count = (wide.shape[1] - 2 * MARGIN) // piece
     total = count * piece
     at = pl.program_id(0)
 
@@ -265,47 +290,75 @@
             lines = dot(pick_ref[pl.ds(r * 2 * owned, 2 * owned), :], rows_ref[...])
             wide[:, MARGIN + r * piece : MARGIN + (r + 1) * piece] = lines.astype(jnp.bfloat16)
 
-    spread = 2 * LANES // SPACING
-    lane = lax.broadcasted_iota(jnp.int32, (2 * spread, 2 * LANES), 1) // SPACING
-    chip = lax.broadcasted_iota(jnp.int32, (2 * spread, 2 * LANES), 0) % spread
-    expand = (lane == chip).astype(jnp.bfloat16)
     first = at * piece
-    for b in range(piece // (2 * LANES)):
-        turn = dot(turn_ref[0, b], expand)
-        for h in range(2):
-            k = 2 * b + h
-            window = wide[:, pl.ds(pl.multiple_of(first + k * LANES, LANES), 2 * LANES)]
-            s = dot(window, band_ref[k])
-            cosine = turn[:owned, h * LANES : (h + 1) * LANES]
-            sine = turn[owned:, h * LANES : (h + 1) * LANES]
-            s_re, s_im = s[:owned], s[owned:]
-            out_ref[0, :, k * LANES : (k + 1) * LANES] = (s_re * cosine + s_im * sine).astype(
-                jnp.bfloat16
-            )
-            out_ref[1, :, k * LANES : (k + 1) * LANES] = (s_im * cosine - s_re * sine).astype(
-                jnp.bfloat16
-            )
-
-
-def finish(pick, rows, bands, turns, owner_cap):
+    for k in range(piece // LANES):
+        window = wide[:, pl.ds(pl.multiple_of(first + k * LANES, LANES), 2 * LANES)]
+        s = dot(window, band_ref[k])
+        out_ref[0, :, k * LANES : (k + 1) * LANES] = s[:owned]
+        out_ref[1, :, k * LANES : (k + 1) * LANES] = s[owned:]
+
+
+def resample(pick, rows, bands, owner_cap):
     piece = rows.shape[1]
-    count = turns.shape[0]
     blocks = piece // LANES
+    count = bands.shape[0] // blocks
     return pl.pallas_call(
-        finish_kernel,
+        resample_kernel,
         grid=(count,),
         in_specs=[
             pl.BlockSpec(pick.shape, lambda i: (0, 0)),
             pl.BlockSpec(rows.shape, lambda i: (0, 0)),
             pl.BlockSpec((blocks, 2 * LANES, LANES), lambda i: (i, 0, 0)),
-            pl.BlockSpec((1,) + turns.shape[1:], lambda i: (i, 0, 0, 0)),
         ],
         out_specs=pl.BlockSpec((2, owner_cap, piece), lambda i: (0, 0, i)),
-        out_shape=jax.ShapeDtypeStruct((2, owner_cap, count * piece), jnp.bfloat16),
+        out_shape=jax.ShapeDtypeStruct((2, owner_cap, count * piece), jnp.float32),
         scratch_shapes=[pltpu.VMEM((2 * owner_cap, count * piece + 2 * MARGIN), jnp.bfloat16)],
         compiler_params=pltpu.CompilerParams(vmem_limit_bytes=VMEM_LIMIT),
-        name="finish_lines",
-    )(pick, rows, bands, turns)
+        cost_estimate=pl.CostEstimate(
+            flops=6_000_000_000, bytes_accessed=12_000_000, transcendentals=0
+        ),
+        name="resample",
+    )(pick, rows, bands)
+
+
+def rotate_kernel(tile_ref, est_ref, lines_ref, out_ref):
+    owned = out_ref.shape[1]
+    count = pl.num_programs(0)
+    at = pl.program_id(0)
+    tiles = est_ref.shape[0] // count
+    tile = tile_ref[...]
+    shift = jnp.zeros((owned, LANES), jnp.float32)
+    for a in range(tiles):
+        shift = jnp.where(tile == a, est_ref[pl.ds(a * count + at, 1), :], shift)
+    angle = PHASE_RATE * shift
+    cosine = jnp.cos(angle)
+    sine = jnp.sin(angle)
+    lane = lax.broadcasted_iota(jnp.int32, (owned, LANES), 1) // SPACING
+    for k in range(out_ref.shape[2] // LANES):
+        chip = lane + k * (LANES // SPACING)
+        cos_k = jnp.take_along_axis(cosine, chip, axis=1)
+        sin_k = jnp.take_along_axis(sine, chip, axis=1)
+        cols = slice(k * LANES, (k + 1) * LANES)
+        s_re = lines_ref[0, :, cols]
+        s_im = lines_ref[1, :, cols]
+        out_ref[0, :, cols] = (s_re * cos_k + s_im * sin_k).astype(jnp.bfloat16)
+        out_ref[1, :, cols] = (s_im * cos_k - s_re * sin_k).astype(jnp.bfloat16)
+
+
+def rotate(tile, est, lines, count):
+    piece = lines.shape[2] // count
+    return pl.pallas_call(
+        rotate_kernel,
+        grid=(count,),
+        in_specs=[
+            pl.BlockSpec(tile.shape, lambda i: (0, 0)),
+            pl.BlockSpec(est.shape, lambda i: (0, 0)),
+            pl.BlockSpec((2, lines.shape[1], piece), lambda i: (0, 0, i)),
+        ],
+        out_specs=pl.BlockSpec((2, lines.shape[1], piece), lambda i: (0, 0, i)),
+        out_shape=jax.ShapeDtypeStruct(lines.shape, jnp.bfloat16),
+        name="rotate",
+    )(tile, est, lines)
 
 
 def per_device(
@@ -321,11 +374,27 @@
     pair_cap = max(2, (lines_dev + 2 * MAX_SHIFT + owners - 1) // owners)
     owner_cap = pair_cap * az_count
     total_cols = cols_dev * rg_count
-    rim = (CHIP_LEN - SPACING) // 2
     first_row = lines_dev // 2 - CHIP_LEN // 2
     az_index = lax.axis_index("az")
     rg_index = lax.axis_index("rg")
     me_owner = az_index * rg_count + rg_index
+
+    low_rows = secondary_slc[:, lines_dev - MARGIN :, :]
+    top_rows = secondary_slc[:, :MARGIN, :]
+    last = cols_dev - MARGIN
+    edges = jnp.concatenate(
+        [secondary_slc, reference_slc[:, first_row : first_row + CHIP_LEN, :]], axis=1
+    )
+    halos = (
+        moved(low_rows, 1, 0),
+        moved(top_rows, -1, 0),
+        moved(edges[:, :, last:], 0, 1),
+        moved(edges[:, :, :MARGIN], 0, -1),
+        moved(low_rows[:, :, last:], 1, 1),
+        moved(low_rows[:, :, :MARGIN], 1, -1),
+        moved(top_rows[:, :, last:], -1, 1),
+        moved(top_rows[:, :, :MARGIN], -1, -1),
+    )
 
     count = src_row.shape[0]
     ids = jnp.arange(count, dtype=jnp.int32)
@@ -348,42 +417,23 @@
         target[:, None] == jnp.arange(2 * lines_dev, dtype=jnp.int32)[None, :]
     ).astype(jnp.bfloat16)
     outgoing = gather_rows(send_pick, secondary_slc)
-    arrived = lax.all_to_all(outgoing, ("az", "rg"), split_axis=0, concat_axis=0, tiled=True)
-
-    ref_rows = reference_slc[:, first_row : first_row + CHIP_LEN, :]
-    ref_sides = (
-        shifted(ref_rows[:, :, cols_dev - rim :], "rg", True),
-        shifted(ref_rows[:, :, :rim], "rg", False),
-    )
-    sec_rows = (
-        shifted(secondary_slc[:, lines_dev - MARGIN :, :], "az", True),
-        shifted(secondary_slc[:, :MARGIN, :], "az", False),
-    )
-    tall_right = jnp.concatenate(
-        [a[:, :, cols_dev - MARGIN :] for a in (sec_rows[0], secondary_slc, sec_rows[1])], axis=1
-    )
-    tall_left = jnp.concatenate(
-        [a[:, :, :MARGIN] for a in (sec_rows[0], secondary_slc, sec_rows[1])], axis=1
-    )
-    sec_sides = (shifted(tall_right, "rg", True), shifted(tall_left, "rg", False))
+    with jax.named_scope("exchange"):
+        arrived = lax.all_to_all(
+            outgoing, ("az", "rg"), split_axis=0, concat_axis=0, tiled=True
+        )
 
     offsets = chip_offsets[:, 0]
-    sums = estimate_sums(
-        offsets, reference_slc, ref_sides, secondary_slc, sec_rows, sec_sides, tables
-    )
-    sums = jnp.moveaxis(sums, 1, 0).reshape(2, chip_count, CHIP_LEN)
-    lag_wide = jnp.asarray(np.pad(tables[4], (0, CHIP_LEN - LAG_COUNT)))
-    totals = jnp.sum(sums[0], axis=1) + EPS
-    cent_az = jnp.sum(sums[1], axis=1) / totals
-    cent_rg = jnp.sum(sums[0] * lag_wide[None, :], axis=1) / totals
-    est = jnp.stack([cent_az, cent_rg]) + offsets.astype(jnp.float32)
-    everywhere = lax.all_to_all(
-        jnp.broadcast_to(est[0][None], (owners, chip_count)),
-        ("az", "rg"),
-        split_axis=0,
-        concat_axis=0,
-        tiled=True,
-    ).reshape(az_count, rg_count, chip_count)
+    with jax.named_scope("estimate"):
+        shifts = estimate_shifts(offsets, reference_slc, secondary_slc, halos, tables)
+    est = shifts.reshape(2, chip_count) + offsets.astype(jnp.float32)
+    with jax.named_scope("spread"):
+        everywhere = lax.all_to_all(
+            jnp.broadcast_to(jnp.pad(est[:1], ((0, 0), (0, LANES - chip_count))), (owners, LANES)),
+            ("az", "rg"),
+            split_axis=0,
+            concat_axis=0,
+            tiled=True,
+        )
 
     all_cols = jnp.arange(total_cols, dtype=jnp.int32)
     rel = (band_start - all_cols // LANES * LANES + MARGIN)[None, :]
@@ -404,25 +454,9 @@
         source[:, None] == jnp.arange(owners * 2 * pair_cap, dtype=jnp.int32)[None, :]
     ).astype(jnp.bfloat16)
 
-    tiles = jnp.arange(az_count, dtype=jnp.int32)
-    chosen = jnp.sum(
-        jnp.where(
-            (tile[:, None] == tiles[None, :])[:, :, None, None], everywhere[None], 0.0
-        ),
-        axis=1,
-    )
-    angle = PHASE_RATE * chosen
-    spread = 2 * LANES // SPACING
-    turns = jnp.stack([jnp.cos(angle), jnp.sin(angle)])
-    high = turns.astype(jnp.bfloat16)
-    low = (turns - high.astype(jnp.float32)).astype(jnp.bfloat16)
-    turns = jnp.stack([high, low], axis=0).reshape(
-        2, 2, owner_cap, rg_count, chip_count // spread, spread
-    )
-    turns = turns.transpose(3, 4, 1, 2, 0, 5).reshape(
-        rg_count, chip_count // spread, 2 * owner_cap, 2 * spread
-    )
-    lines_out = finish(recv_pick, arrived, bands, turns, owner_cap)
+    lines = resample(recv_pick, arrived, bands, owner_cap)
+    tile_wide = jnp.broadcast_to(tile[:, None], (owner_cap, LANES))
+    lines_out = rotate(tile_wide, everywhere, lines, rg_count)
     return (est[:, None, :], lines_out)
 
 

time: 116 us -> 106 us (0.914)
  waiting for transfers between devices: 39.8 us -> 4.69 us
  starting transfers between devices: 27.8 us -> 48 us
  Pallas kernels: 31.9 us -> 36.9 us
  local copies, waits for them, and re-layouts: 9.49 us -> 6.26 us
  other arithmetic: 4.64 us -> 7.3 us
    all_to_all x1, waiting for transfers between devices: 22.1 us -> 0.01 us  [per_device(): lax.all_to_all(outgoing, ('az', 'rg'), split_axis=0, concat_axis=0, tiled...]
    ppermute x6 -> x8, starting transfers between devices: 16.8 us -> 32.1 us  [moved(): return lax.ppermute(cells, ('az', 'rg'), pairs)]
    ppermute x6 -> x8, waiting for transfers between devices: 14.5 us -> 4.68 us  [moved(): return lax.ppermute(cells, ('az', 'rg'), pairs)]
    pallas_call x2 -> x3, Pallas kernels: 18.2 us -> 23.1 us  [the longest x1 11 us: estimate_shifts(): pl.pallas_call(estimate_kernel, in_specs=[pl.BlockSpec(memory_space=pltpu...]
    all_to_all x1, starting transfers between devices: 3.03 us -> 7.08 us  [per_device(): lax.all_to_all(outgoing, ('az', 'rg'), split_axis=0, concat_axis=0, tiled...]
    all_to_all x1, waiting for transfers between devices: 3.09 us -> 0.01 us  [per_device(): lax.all_to_all(jnp.broadcast_to(jnp.pad(est[:1], ((0, 0), (0, LANES - chi...]
    slice x7 -> x5, local copies, waits for them, and re-layouts: 4.43 us -> 2.14 us  [the longest x1 1.41 us: per_device(): top_rows = secondary_slc[:, :MARGIN, :]]
  transfers between devices with their start and end apart: 8 -> 10, of which waited for: 4 -> 1; matrix products, arithmetic and copies ran while one was open for 8% -> 7% of each run, Pallas kernels for 12% -> 27%
where the time goes in v1:
time: 106 us; the launch traced here: 104 us
  starting transfers between devices  48 us (45%)
  Pallas kernels  36.9 us (35%)
  other arithmetic  7.3 us (7%)
  local copies, waits for them, and re-layouts  6.26 us (6%)
  waiting for transfers between devices  4.69 us (4%)
    ppermute x8, starting transfers between devices, moved(): return lax.ppermute(cells, ('az', 'rg'), pairs)  32.1 us
    pallas_call x1, Pallas kernels, estimate_shifts(): pl.pallas_call(estimate_kernel, in_specs=[pl.BlockSpec(memory_space=pltpu...  11 us
    pallas_call x1, Pallas kernels, build_bands(): pl.pallas_call(band_kernel, grid=(count // step,), in_specs=[pl.BlockSpec...  10.1 us
    all_to_all x1, starting transfers between devices, per_device(): lax.all_to_all(jnp.broadcast_to(jnp.pad(est[:1], ((0, 0), (0, LANES - chi...  8.79 us
    pallas_call x1, Pallas kernels, resample(): pl.pallas_call(resample_kernel, grid=(count,), in_specs=[pl.BlockSpec(pic...  7.47 us
    all_to_all x1, starting transfers between devices, per_device(): lax.all_to_all(outgoing, ('az', 'rg'), split_axis=0, concat_axis=0, tiled...  7.08 us
    ppermute x8, waiting for transfers between devices, moved(): return lax.ppermute(cells, ('az', 'rg'), pairs)  4.68 us
    pallas_call x1, Pallas kernels, rotate(): pl.pallas_call(rotate_kernel, grid=(count,), in_specs=[pl.BlockSpec(tile....  4.66 us
  transfers between devices with their start and end apart: 10, of which 1 were waited for; matrix products, arithmetic and copies ran while one was open for 7% of the time, Pallas kernels for 27%

profile of v1, /device:TPU:1, one launch (start us, length us, event | category | flops | bytes accessed | tf_op | source)
XLA Modules:
  0.0 104.1 jit_solution(2496354466385702466)
XLA Ops:
  0.6 0.7 add_select_fusion.2
  1.3 1.2 %convert_reduce_fusion.1 = (s32[768]{0:T(1024)S(1)}, s32[768]{0:T(1024)S(1)}) fusion(s32[768]{0:T(1024)} %param.17, s32[768]{0:T(1024)S(1)} %add_select_fusion.2), kind=kLoop, calls=%fused_computation.1 | loop fusion | flops 5306880 | bytes 12288 | tf_op jit(solution)/shard_map/reduce_sum | solution.py:403
  2.6 0.7 add_select_fusion.3
  3.3 0.1 select_reduce_fusion
  3.4 0.1 sub.43
  3.6 0.1 add_select_fusion.1
  3.6 0.1 select_n.77
  3.8 0.8 fusion.2.pick_ref
  4.5 0.0 copy-start
  4.5 3.7 %gather_rows.1 = bf16[256,3072]{1,0:T(8,128)(2,1)} custom-call(bf16[256,192]{1,0:T(8,128)(2,1)} %fusion.2.pick_ref, bf16[2,96,3072]{2,1,0:T(8,128)(2,1)} %rows_ref.1), custom_call_target="tpu_custom_call" | custom-call | tf_op jit(solution)/shard_map/gather_rows/pallas_call | solution.py:89
  8.2 7.1 %all-to-all-start.1 = ((bf16[32,8,3072]{2,1,0:T(8,128)(2,1)}), bf16[32,8,3072]{2,1,0:T(8,128)(2,1)S(1)}, u32[]{:S(2)}, u32[]{:S(2)}) async-start(bf16[32,8,3072]{2,1,0:T(8,128)(2,1)} %bitcast.9), calls=%async_computation.1 | async-start | bytes 3145728 | tf_op jit(solution)/shard_map/exchange/all_to_all | solution.py:421
  15.3 0.0 copy-done
  15.3 0.0 copy-start.3
  15.3 0.7 fusion.11
  16.0 5.0 %collective-permute-start.4 = (bf16[2,64,64]{2,1,0:T(8,128)(2,1)}, bf16[2,64,64]{2,1,0:T(8,128)(2,1)}, u32[]{:S(2)}, u32[]{:S(2)}) collective-permute-start(bf16[2,64,64]{2,1,0:T(8,128)(2,1)} %get-tuple-element.18), channel_id=1, source_target_pairs={{0,5},{1,6},{2,7},{4,9},{5,10},{6,11},{8,13},{9,14},{10,15},{12,17... | collective-permute-start | bytes 49160 | tf_op jit(solution)/shard_map/ppermute | solution.py:36
  21.1 1.3 %collective-permute-start.5 = (bf16[2,64,64]{2,1,0:T(8,128)(2,1)}, bf16[2,64,64]{2,1,0:T(8,128)(2,1)}, u32[]{:S(2)}, u32[]{:S(2)}) collective-permute-start(bf16[2,64,64]{2,1,0:T(8,128)(2,1)} %get-tuple-element.17), channel_id=1, source_target_pairs={{1,4},{2,5},{3,6},{5,8},{6,9},{7,10},{9,12},{10,13},{11,14},{13,16... | collective-permute-start | bytes 49160 | tf_op jit(solution)/shard_map/ppermute | solution.py:36
  22.4 0.0 slice-start
  22.4 5.6 %collective-permute-start.6 = (bf16[2,64,64]{2,1,0:T(8,128)(2,1)}, bf16[2,64,64]{2,1,0:T(8,128)(2,1)}, u32[]{:S(2)}, u32[]{:S(2)}) collective-permute-start(bf16[2,64,64]{2,1,0:T(8,128)(2,1)} %get-tuple-element.16), channel_id=1, source_target_pairs={{4,1},{5,2},{6,3},{8,5},{9,6},{10,7},{12,9},{13,10},{14,11},{16,13... | collective-permute-start | bytes 49160 | tf_op jit(solution)/shard_map/ppermute | solution.py:36
  28.0 1.4 %fusion.12 = (bf16[2,64,3072]{2,1,0:T(8,128)(2,1)}, bf16[2,64,3072]{2,1,0:T(8,128)(2,1)}) fusion(bf16[2,96,3072]{2,1,0:T(8,128)(2,1)S(1)} %copy-done), kind=kLoop, calls=%fused_computation.51 | loop fusion | bytes 3145728 | tf_op jit(solution)/shard_map/slice | solution.py:383
  29.4 2.5 %collective-permute-start = (bf16[2,64,3072]{2,1,0:T(8,128)(2,1)}, bf16[2,64,3072]{2,1,0:T(8,128)(2,1)}, u32[]{:S(2)}, u32[]{:S(2)}) collective-permute-start(bf16[2,64,3072]{2,1,0:T(8,128)(2,1)} %get-tuple-element.20), channel_id=1, source_target_pairs={{0,4},{1,5},{2,6},{3,7},{4,8},{5,9},{6,10},{7,11},{8,12},{9,13},{1... | collective-permute-start | bytes 2359304 | tf_op jit(solution)/shard_map/ppermute | solution.py:36
  31.9 2.7 %collective-permute-start.1 = (bf16[2,64,3072]{2,1,0:T(8,128)(2,1)}, bf16[2,64,3072]{2,1,0:T(8,128)(2,1)}, u32[]{:S(2)}, u32[]{:S(2)}) collective-permute-start(bf16[2,64,3072]{2,1,0:T(8,128)(2,1)} %get-tuple-element.19), channel_id=1, source_target_pairs={{4,0},{5,1},{6,2},{7,3},{8,4},{9,5},{10,6},{11,7},{12,8},{13,9},{1... | collective-permute-start | bytes 2359304 | tf_op jit(solution)/shard_map/ppermute | solution.py:36
  34.6 0.0 copy-done.3
  34.6 0.1 select_reduce_fusion.1
  34.8 1.4 %fusion.6 = s32[12288]{0:T(1024)} fusion(s32[12288]{0:T(1024)} %param.18), kind=kLoop, calls=%fused_computation.21 | loop fusion | flops 135168 | bytes 98304 | tf_op jit(solution)/shard_map/add | solution.py:439
  36.2 0.0 slice-done
  36.3 0.7 pad_maximum_fusion
  37.0 0.1 select_n.73
  37.1 4.7 %collective-permute-done.4.top_left = bf16[2,64,64]{2,1,0:T(8,128)(2,1)} collective-permute-done((bf16[2,64,64]{2,1,0:T(8,128)(2,1)}, bf16[2,64,64]{2,1,0:T(8,128)(2,1)}, u32[]{:S(2)}, u32[]{:S(2)}) %collective-permute-start.4) | collective-permute-done | bytes 16416 | tf_op jit(solution)/shard_map/ppermute | solution.py:36
  41.7 1.3 %collective-permute-start.7 = (bf16[2,64,64]{2,1,0:T(8,128)(2,1)}, bf16[2,64,64]{2,1,0:T(8,128)(2,1)S(1)}, u32[]{:S(2)}, u32[]{:S(2)}) collective-permute-start(bf16[2,64,64]{2,1,0:T(8,128)(2,1)} %get-tuple-element.15), channel_id=1, source_target_pairs={{5,0},{6,1},{7,2},{9,4},{10,5},{11,6},{13,8},{14,9},{15,10},{17,12... | collective-permute-start | bytes 49160 | tf_op jit(solution)/shard_map/ppermute | solution.py:36
  43.0 0.0 collective-permute-done.5.top_right
  43.0 12.5 %collective-permute-start.2 = (bf16[2,160,64]{2,1,0:T(8,128)(2,1)}, bf16[2,160,64]{2,1,0:T(8,128)(2,1)S(1)}, u32[]{:S(2)}, u32[]{:S(2)}) collective-permute-start(bf16[2,160,64]{2,1,0:T(8,128)(2,1)} %get-tuple-element.14), channel_id=1, source_target_pairs={{0,1},{1,2},{2,3},{4,5},{5,6},{6,7},{8,9},{9,10},{10,11},{12,13},{... | collective-permute-start | bytes 122888 | tf_op jit(solution)/shard_map/ppermute | solution.py:36
  55.5 0.0 collective-permute-done.6.low_left
  55.5 1.3 %collective-permute-start.3 = (bf16[2,160,64]{2,1,0:T(8,128)(2,1)}, bf16[2,160,64]{2,1,0:T(8,128)(2,1)S(1)}, u32[]{:S(2)}, u32[]{:S(2)}) collective-permute-start(bf16[2,160,64]{2,1,0:T(8,128)(2,1)} %get-tuple-element.13), channel_id=1, source_target_pairs={{1,0},{2,1},{3,2},{5,4},{6,5},{7,6},{9,8},{10,9},{11,10},{13,12},{... | collective-permute-start | bytes 122888 | tf_op jit(solution)/shard_map/ppermute | solution.py:36
  56.8 0.8 fusion.1.pick_ref
  57.6 10.1 %build_bands.1.band_ref = bf16[96,256,128]{2,1,0:T(8,128)(2,1)} custom-call(s32[1,12288]{1,0:T(1,128)} %bitcast.11, bf16[8,12288]{1,0:T(8,128)(2,1)} %taps_ref.1), custom_call_target="tpu_custom_call" | custom-call | flops 100663296 | bytes 6291456 | tf_op jit(solution)/shard_map/build_bands/pallas_call | solution.py:118
  67.7 0.0 collective-permute-done.7.low_right
  67.7 0.0 copy-start.7
  67.7 0.0 collective-permute-done.2.left
  67.7 0.0 copy-start.5
  67.7 0.0 collective-permute-done.3.right
  67.7 0.0 copy-start.6
  67.7 0.0 collective-permute-done.sec_top
  67.8 0.0 collective-permute-done.1.sec_low
  67.8 0.5 copy-done.7
  68.3 0.0 copy-done.5
  68.3 0.0 copy-done.6
  68.4 0.0 copy-start.4
  68.4 11.0 %estimate_shifts.1 = f32[2,48,2]{2,1,0:T(8,128)} custom-call(s32[2,96]{1,0:T(2,128)} %bitcast.13, bf16[2,96,3072]{2,1,0:T(8,128)(2,1)} %ref_ref.1, bf16[2,96,3072]{2,1,0:T(8,128)(2,1)} %rows_ref.1, bf16[2,64,3072]{2,1,0:T(8,128)(2,1)} %collective-permute-done.sec_top, bf16[2,64,3072]{2,1,0:T(8,128)(2,1)} %collective-permute-done.1.sec_low, ...), custom_call_target="tpu_custom_call" | custom-call | flops 10000000000 | bytes 8000000 | tf_op jit(solution)/shard_map/estimate/estimate_shifts/pallas_call | solution.py:258
  79.3 0.9 reshape.185
  80.3 0.9 reshape.184
  81.2 0.0 copy-done.4
  81.2 0.6 convert_add_fusion.1
  81.8 0.0 all-to-all-done.1
  81.8 0.0 copy-start.1
  81.8 0.7 broadcast_in_dim.62
  82.5 8.8 %all-to-all-start = ((f32[32,1,128]{2,1,0:T(1,128)}), f32[32,1,128]{2,1,0:T(1,128)S(1)}, u32[]{:S(2)}, u32[]{:S(2)}) async-start(f32[32,1,128]{2,1,0:T(1,128)} %broadcast_in_dim.62), calls=%async_computation | async-start | bytes 32768 | tf_op jit(solution)/shard_map/spread/all_to_all | solution.py:430
  91.3 0.0 copy-done.1
  91.3 7.5 %resample.1.lines_ref = f32[2,32,12288]{2,1,0:T(8,128)} custom-call(bf16[256,256]{1,0:T(8,128)(2,1)} %fusion.1.pick_ref, bf16[256,3072]{1,0:T(8,128)(2,1)} %bitcast.10, bf16[96,256,128]{2,1,0:T(8,128)(2,1)} %build_bands.1.band_ref), custom_call_target="tpu_custom_call" | custom-call | flops 6000000000 | bytes 12000000 | tf_op jit(solution)/shard_map/resample/pallas_call | solution.py:305
  98.8 0.0 all-to-all-done
  98.8 0.0 copy-start.2
  98.8 0.7 broadcast_in_dim.61.tile_ref
  99.4 0.0 copy-done.2
  99.4 4.7 %rotate.1 = bf16[2,32,12288]{2,1,0:T(8,128)(2,1)} custom-call(s32[32,128]{1,0:T(8,128)} %broadcast_in_dim.61.tile_ref, f32[32,128]{1,0:T(8,128)} %bitcast.12, f32[2,32,12288]{2,1,0:T(8,128)} %resample.1.lines_ref), custom_call_target="tpu_custom_call" | custom-call | tf_op jit(solution)/shard_map/rotate/pallas_call | solution.py:350
  (12 shorter events, 0.1 us)
Async XLA Ops:
  4.5 10.8 %copy-start = (bf16[2,96,3072]{2,1,0:T(8,128)(2,1)S(1)}, bf16[2,96,3072]{2,1,0:T(8,128)(2,1)}, u32[]{:S(2)}) copy-start(bf16[2,96,3072]{2,1,0:T(8,128)(2,1)} %rows_ref.1) | copy-start | bytes 3538948
  8.2 73.6 %all-to-all-start.1 = ((bf16[32,8,3072]{2,1,0:T(8,128)(2,1)}), bf16[32,8,3072]{2,1,0:T(8,128)(2,1)S(1)}, u32[]{:S(2)}, u32[]{:S(2)}) async-start(bf16[32,8,3072]{2,1,0:T(8,128)(2,1)} %bitcast.9), calls=%async_computation.1 | async-start | bytes 3145728 | tf_op jit(solution)/shard_map/exchange/all_to_all | solution.py:421
  15.3 19.3 %copy-start.3 = (s32[768]{0:T(1024)S(1)}, s32[768]{0:T(1024)}, u32[]{:S(2)}) copy-start(s32[768]{0:T(1024)} %param.17) | copy-start | bytes 9220
  16.0 25.7 %collective-permute-start.4 = (bf16[2,64,64]{2,1,0:T(8,128)(2,1)}, bf16[2,64,64]{2,1,0:T(8,128)(2,1)}, u32[]{:S(2)}, u32[]{:S(2)}) collective-permute-start(bf16[2,64,64]{2,1,0:T(8,128)(2,1)} %get-tuple-element.18), channel_id=1, source_target_pairs={{0,5},{1,6},{2,7},{4,9},{5,10},{6,11},{8,13},{9,14},{10,15},{12,17... | collective-permute-start | bytes 49160 | tf_op jit(solution)/shard_map/ppermute | solution.py:36
  21.1 21.9 %collective-permute-start.5 = (bf16[2,64,64]{2,1,0:T(8,128)(2,1)}, bf16[2,64,64]{2,1,0:T(8,128)(2,1)}, u32[]{:S(2)}, u32[]{:S(2)}) collective-permute-start(bf16[2,64,64]{2,1,0:T(8,128)(2,1)} %get-tuple-element.17), channel_id=1, source_target_pairs={{1,4},{2,5},{3,6},{5,8},{6,9},{7,10},{9,12},{10,13},{11,14},{13,16... | collective-permute-start | bytes 49160 | tf_op jit(solution)/shard_map/ppermute | solution.py:36
  22.4 13.9 %slice-start = ((bf16[2,96,3072]{2,1,0:T(8,128)(2,1)}), bf16[2,64,3072]{2,1,0:T(8,128)(2,1)S(1)}, s32[]{:S(2)}) async-start(bf16[2,96,3072]{2,1,0:T(8,128)(2,1)} %ref_ref.1), calls=%async_computation.2 | async-start | bytes 1572864 | tf_op jit(solution)/shard_map/slice | solution.py:386
  22.4 33.1 %collective-permute-start.6 = (bf16[2,64,64]{2,1,0:T(8,128)(2,1)}, bf16[2,64,64]{2,1,0:T(8,128)(2,1)}, u32[]{:S(2)}, u32[]{:S(2)}) collective-permute-start(bf16[2,64,64]{2,1,0:T(8,128)(2,1)} %get-tuple-element.16), channel_id=1, source_target_pairs={{4,1},{5,2},{6,3},{8,5},{9,6},{10,7},{12,9},{13,10},{14,11},{16,13... | collective-permute-start | bytes 49160 | tf_op jit(solution)/shard_map/ppermute | solution.py:36
  29.4 38.4 %collective-permute-start = (bf16[2,64,3072]{2,1,0:T(8,128)(2,1)}, bf16[2,64,3072]{2,1,0:T(8,128)(2,1)}, u32[]{:S(2)}, u32[]{:S(2)}) collective-permute-start(bf16[2,64,3072]{2,1,0:T(8,128)(2,1)} %get-tuple-element.20), channel_id=1, source_target_pairs={{0,4},{1,5},{2,6},{3,7},{4,8},{5,9},{6,10},{7,11},{8,12},{9,13},{1... | collective-permute-start | bytes 2359304 | tf_op jit(solution)/shard_map/ppermute | solution.py:36
  31.9 35.9 %collective-permute-start.1 = (bf16[2,64,3072]{2,1,0:T(8,128)(2,1)}, bf16[2,64,3072]{2,1,0:T(8,128)(2,1)}, u32[]{:S(2)}, u32[]{:S(2)}) collective-permute-start(bf16[2,64,3072]{2,1,0:T(8,128)(2,1)} %get-tuple-element.19), channel_id=1, source_target_pairs={{4,0},{5,1},{6,2},{7,3},{8,4},{9,5},{10,6},{11,7},{12,8},{13,9},{1... | collective-permute-start | bytes 2359304 | tf_op jit(solution)/shard_map/ppermute | solution.py:36
  41.7 26.0 %collective-permute-start.7 = (bf16[2,64,64]{2,1,0:T(8,128)(2,1)}, bf16[2,64,64]{2,1,0:T(8,128)(2,1)S(1)}, u32[]{:S(2)}, u32[]{:S(2)}) collective-permute-start(bf16[2,64,64]{2,1,0:T(8,128)(2,1)} %get-tuple-element.15), channel_id=1, source_target_pairs={{5,0},{6,1},{7,2},{9,4},{10,5},{11,6},{13,8},{14,9},{15,10},{17,12... | collective-permute-start | bytes 49160 | tf_op jit(solution)/shard_map/ppermute | solution.py:36
  43.0 24.7 %collective-permute-start.2 = (bf16[2,160,64]{2,1,0:T(8,128)(2,1)}, bf16[2,160,64]{2,1,0:T(8,128)(2,1)S(1)}, u32[]{:S(2)}, u32[]{:S(2)}) collective-permute-start(bf16[2,160,64]{2,1,0:T(8,128)(2,1)} %get-tuple-element.14), channel_id=1, source_target_pairs={{0,1},{1,2},{2,3},{4,5},{5,6},{6,7},{8,9},{9,10},{10,11},{12,13},{... | collective-permute-start | bytes 122888 | tf_op jit(solution)/shard_map/ppermute | solution.py:36
  55.5 12.2 %collective-permute-start.3 = (bf16[2,160,64]{2,1,0:T(8,128)(2,1)}, bf16[2,160,64]{2,1,0:T(8,128)(2,1)S(1)}, u32[]{:S(2)}, u32[]{:S(2)}) collective-permute-start(bf16[2,160,64]{2,1,0:T(8,128)(2,1)} %get-tuple-element.13), channel_id=1, source_target_pairs={{1,0},{2,1},{3,2},{5,4},{6,5},{7,6},{9,8},{10,9},{11,10},{13,12},{... | collective-permute-start | bytes 122888 | tf_op jit(solution)/shard_map/ppermute | solution.py:36
  67.7 0.6 copy-start.7
  67.7 0.6 copy-start.5
  67.7 0.6 copy-start.6
  68.4 12.8 %copy-start.4 = (s32[2,1,96]{2,1,0:T(1,128)S(1)}, s32[2,1,96]{2,1,0:T(1,128)}, u32[]{:S(2)}) copy-start(s32[2,1,96]{2,1,0:T(1,128)} %param.15) | copy-start | bytes 2308
  81.8 9.5 %copy-start.1 = (bf16[32,8,3072]{2,1,0:T(8,128)(2,1)}, bf16[32,8,3072]{2,1,0:T(8,128)(2,1)S(1)}, u32[]{:S(2)}) copy-start(bf16[32,8,3072]{2,1,0:T(8,128)(2,1)S(1)} %all-to-all-done.1) | copy-start | bytes 4718596
  82.5 16.3 %all-to-all-start = ((f32[32,1,128]{2,1,0:T(1,128)}), f32[32,1,128]{2,1,0:T(1,128)S(1)}, u32[]{:S(2)}, u32[]{:S(2)}) async-start(f32[32,1,128]{2,1,0:T(1,128)} %broadcast_in_dim.62), calls=%async_computation | async-start | bytes 32768 | tf_op jit(solution)/shard_map/spread/all_to_all | solution.py:430
  98.8 0.7 copy-start.2

commit v2 on v1

--- a/solution.py
+++ b/solution.py
@@ -1,4 +1,3 @@
-import functools
 import math
 
 import jax
@@ -8,6 +7,7 @@
 from jax.experimental import pallas as pl
 from jax.experimental.pallas import tpu as pltpu
 from jax.sharding import PartitionSpec as P
+
 
 CHIP_LEN = 64
 OVERSAMPLE = 16
@@ -77,7 +77,6 @@
 
 
 def gather_kernel(pick_ref, rows_ref, out_ref):
-    lines = rows_ref.shape[1]
     rows = jnp.concatenate([rows_ref[0], rows_ref[1]], axis=0)
     out_ref[...] = dot(pick_ref[...], rows).astype(jnp.bfloat16)
 
@@ -133,8 +132,8 @@
 
 def estimate_kernel(
     off_ref, ref_ref, sec_ref, sec_top, sec_low, left, right, top_left, top_right, low_left,
-    low_right, four_ref, spec_ref, lift_ref, corr_ref, lag_ref, wide_ref, out_ref, ref_win,
-    sec_win, plain_ref, lagged_ref,
+    low_right, four_ref, spec_ref, lift_ref, corr_ref, lag_ref, wide_ref, base_ref, out_ref,
+    spread_ref, ref_win, sec_win, plain_ref, lagged_ref,
 ):
     lines = sec_ref.shape[1]
     cols = sec_ref.shape[2]
@@ -237,18 +236,21 @@
     plain = plain_ref[...]
     lagged = lagged_ref[...]
     across = plain * wide_ref[...]
+    lane = lax.broadcasted_iota(jnp.int32, (chips // 2, LANES), 1)
+    place = lax.broadcasted_iota(jnp.int32, (chips // 2, LANES), 0) * 2
+    rows = [jnp.zeros((chips // 2, LANES), jnp.float32)] * 2
     for h in range(2):
         inside = near if h == 0 else jnp.logical_not(near)
         total = jnp.sum(jnp.where(inside, plain, 0.0), axis=1, keepdims=True) + EPS
-        out_ref[0, :, h : h + 1] = (
-            jnp.sum(jnp.where(inside, lagged, 0.0), axis=1, keepdims=True) / total
-        )
-        out_ref[1, :, h : h + 1] = (
-            jnp.sum(jnp.where(inside, across, 0.0), axis=1, keepdims=True) / total
-        )
-
-
-def estimate_shifts(offsets, ref, sec, halos, tables):
+        for c, moment in enumerate((lagged, across)):
+            centre = jnp.sum(jnp.where(inside, moment, 0.0), axis=1, keepdims=True) / total
+            rows[c] = jnp.where(lane == place + h, centre, rows[c])
+    for c in range(2):
+        out_ref[c : c + 1, :] = jnp.sum(rows[c], axis=0, keepdims=True) + base_ref[c : c + 1, :]
+    spread_ref[...] = jnp.broadcast_to(out_ref[0:1, :], spread_ref.shape)
+
+
+def estimate_shifts(offsets, ref, sec, halos, tables, owners):
     four, spec, lift, corr, lags = tables
     lines = sec.shape[1]
     chips = sec.shape[2] // SPACING
@@ -257,9 +259,12 @@
     lag_wide = np.tile(np.pad(lags, (0, CHIP_LEN - LAG_COUNT)), 2)[None, :]
     return pl.pallas_call(
         estimate_kernel,
-        in_specs=[pl.BlockSpec(memory_space=pltpu.SMEM)] + [vmem] * 16,
-        out_specs=vmem,
-        out_shape=jax.ShapeDtypeStruct((2, chips // 2, 2), jnp.float32),
+        in_specs=[pl.BlockSpec(memory_space=pltpu.SMEM)] + [vmem] * 17,
+        out_specs=(vmem, vmem),
+        out_shape=(
+            jax.ShapeDtypeStruct((2, LANES), jnp.float32),
+            jax.ShapeDtypeStruct((owners, LANES), jnp.float32),
+        ),
         scratch_shapes=[
             pltpu.VMEM((2, blocks, CHIP_LEN, LANES), jnp.float32),
             pltpu.VMEM((2, blocks, lines + 2 * MARGIN, LANES), jnp.float32),
@@ -272,7 +277,7 @@
         ),
         name="estimate_shifts",
     )(offsets, ref, sec, *halos, four, spec, lift, corr, jnp.asarray(lags)[:, None],
-      jnp.asarray(lag_wide))
+      jnp.asarray(lag_wide), jnp.pad(offsets, ((0, 0), (0, LANES - chips))).astype(jnp.float32))
 
 
 def resample_kernel(pick_ref, rows_ref, band_ref, out_ref, wide):
@@ -321,18 +326,24 @@
     )(pick, rows, bands)
 
 
-def rotate_kernel(tile_ref, est_ref, lines_ref, out_ref):
+def rotate_kernel(tile_ref, est_ref, lines_ref, out_ref, turns):
     owned = out_ref.shape[1]
     count = pl.num_programs(0)
     at = pl.program_id(0)
     tiles = est_ref.shape[0] // count
     tile = tile_ref[...]
-    shift = jnp.zeros((owned, LANES), jnp.float32)
+
+    @pl.when(at == 0)
+    def _():
+        angle = PHASE_RATE * est_ref[...]
+        turns[0] = jnp.cos(angle)
+        turns[1] = jnp.sin(angle)
+
+    cosine = jnp.zeros((owned, LANES), jnp.float32)
+    sine = jnp.zeros((owned, LANES), jnp.float32)
     for a in range(tiles):
-        shift = jnp.where(tile == a, est_ref[pl.ds(a * count + at, 1), :], shift)
-    angle = PHASE_RATE * shift
-    cosine = jnp.cos(angle)
-    sine = jnp.sin(angle)
+        cosine = jnp.where(tile == a, turns[0, pl.ds(a * count + at, 1), :], cosine)
+        sine = jnp.where(tile == a, turns[1, pl.ds(a * count + at, 1), :], sine)
     lane = lax.broadcasted_iota(jnp.int32, (owned, LANES), 1) // SPACING
     for k in range(out_ref.shape[2] // LANES):
         chip = lane + k * (LANES // SPACING)
@@ -357,6 +368,7 @@
         ],
         out_specs=pl.BlockSpec((2, lines.shape[1], piece), lambda i: (0, 0, i)),
         out_shape=jax.ShapeDtypeStruct(lines.shape, jnp.bfloat16),
+        scratch_shapes=[pltpu.VMEM((2,) + est.shape, jnp.float32)],
         name="rotate",
     )(tile, est, lines)
 
@@ -385,16 +397,19 @@
     edges = jnp.concatenate(
         [secondary_slc, reference_slc[:, first_row : first_row + CHIP_LEN, :]], axis=1
     )
-    halos = (
-        moved(low_rows, 1, 0),
-        moved(top_rows, -1, 0),
-        moved(edges[:, :, last:], 0, 1),
-        moved(edges[:, :, :MARGIN], 0, -1),
-        moved(low_rows[:, :, last:], 1, 1),
-        moved(low_rows[:, :, :MARGIN], 1, -1),
-        moved(top_rows[:, :, last:], -1, 1),
-        moved(top_rows[:, :, :MARGIN], -1, -1),
-    )
+    sends = (
+        (low_rows, 1, 0),
+        (top_rows, -1, 0),
+        (edges[:, :, last:], 0, 1),
+        (edges[:, :, :MARGIN], 0, -1),
+        (low_rows[:, :, last:], 1, 1),
+        (low_rows[:, :, :MARGIN], 1, -1),
+        (top_rows[:, :, last:], -1, 1),
+        (top_rows[:, :, :MARGIN], -1, -1),
+    )
+    halos = []
+    for which, send in enumerate(sends):
+        halos.append(moved(*send))
 
     count = src_row.shape[0]
     ids = jnp.arange(count, dtype=jnp.int32)
@@ -417,23 +432,22 @@
         target[:, None] == jnp.arange(2 * lines_dev, dtype=jnp.int32)[None, :]
     ).astype(jnp.bfloat16)
     outgoing = gather_rows(send_pick, secondary_slc)
-    with jax.named_scope("exchange"):
-        arrived = lax.all_to_all(
-            outgoing, ("az", "rg"), split_axis=0, concat_axis=0, tiled=True
-        )
+    arrived = lax.all_to_all(
+        outgoing, ("az", "rg"), split_axis=0, concat_axis=0, tiled=True
+    )
 
     offsets = chip_offsets[:, 0]
-    with jax.named_scope("estimate"):
-        shifts = estimate_shifts(offsets, reference_slc, secondary_slc, halos, tables)
-    est = shifts.reshape(2, chip_count) + offsets.astype(jnp.float32)
-    with jax.named_scope("spread"):
-        everywhere = lax.all_to_all(
-            jnp.broadcast_to(jnp.pad(est[:1], ((0, 0), (0, LANES - chip_count))), (owners, LANES)),
-            ("az", "rg"),
-            split_axis=0,
-            concat_axis=0,
-            tiled=True,
-        )
+    est, spread = estimate_shifts(
+        offsets, reference_slc, secondary_slc, halos, tables, owners
+    )
+    est = est[:, :chip_count]
+    everywhere = lax.all_to_all(
+        spread,
+        ("az", "rg"),
+        split_axis=0,
+        concat_axis=0,
+        tiled=True,
+    )
 
     all_cols = jnp.arange(total_cols, dtype=jnp.int32)
     rel = (band_start - all_cols // LANES * LANES + MARGIN)[None, :]

time: 106 us -> 102 us (0.962)
  local copies, waits for them, and re-layouts: 6.26 us -> 3.76 us
    reshape x2 -> x0, local copies, waits for them, and re-layouts: 1.83 us -> none  [per_device(): est = shifts.reshape(2, chip_count) + offsets.astype(jnp.float32)]
  transfers between devices with their start and end apart: 10 -> 10, of which waited for: 1 -> 1; matrix products, arithmetic and copies ran while one was open for 7% -> 6% of each run, Pallas kernels for 27% -> 28%
where the time goes in v2:
time: 102 us; the launch traced here: 101 us
  starting transfers between devices  48.2 us (47%)
  Pallas kernels  36.8 us (36%)
  other arithmetic  7.33 us (7%)
  local copies, waits for them, and re-layouts  3.76 us (4%)
  waiting for transfers between devices  3.75 us (4%)
    ppermute x8, starting transfers between devices, moved(): return lax.ppermute(cells, ('az', 'rg'), pairs)  32.3 us
    pallas_call x1, Pallas kernels, estimate_shifts(): pl.pallas_call(estimate_kernel, in_specs=[pl.BlockSpec(memory_space=pltpu...  11 us
    pallas_call x1, Pallas kernels, build_bands(): pl.pallas_call(band_kernel, grid=(count // step,), in_specs=[pl.BlockSpec...  10.1 us
    all_to_all x1, starting transfers between devices, per_device(): lax.all_to_all(spread, ('az', 'rg'), split_axis=0, concat_axis=0, tiled=T...  8.79 us
    pallas_call x1, Pallas kernels, resample(): pl.pallas_call(resample_kernel, grid=(count,), in_specs=[pl.BlockSpec(pic...  7.46 us
    all_to_all x1, starting transfers between devices, per_device(): lax.all_to_all(outgoing, ('az', 'rg'), split_axis=0, concat_axis=0, tiled...  7.09 us
    pallas_call x1, Pallas kernels, rotate(): pl.pallas_call(rotate_kernel, grid=(count,), in_specs=[pl.BlockSpec(tile....  4.6 us
    ppermute x8, waiting for transfers between devices, moved(): return lax.ppermute(cells, ('az', 'rg'), pairs)  3.74 us
  transfers between devices with their start and end apart: 10, of which 1 were waited for; matrix products, arithmetic and copies ran while one was open for 6% of the time, Pallas kernels for 28%

profile of v2, /device:TPU:1, one launch (start us, length us, event | category | flops | bytes accessed | tf_op | source)
XLA Modules:
  0.0 100.7 jit_solution(4184162803147537410)
XLA Ops:
  0.6 0.7 add_select_fusion.2
  1.3 1.2 %convert_reduce_fusion.1 = (s32[768]{0:T(1024)S(1)}, s32[768]{0:T(1024)S(1)}) fusion(s32[768]{0:T(1024)} %param.17, s32[768]{0:T(1024)S(1)} %add_select_fusion.2), kind=kLoop, calls=%fused_computation.1 | loop fusion | flops 5306880 | bytes 12288 | tf_op jit(solution)/shard_map/reduce_sum | solution.py:418
  2.6 0.7 add_select_fusion.3
  3.3 0.1 select_reduce_fusion
  3.4 0.1 sub.43
  3.6 0.1 add_select_fusion.1
  3.6 0.1 select_n.77
  3.8 0.8 fusion.2.pick_ref
  4.5 0.0 copy-start
  4.5 3.7 %gather_rows.1 = bf16[256,3072]{1,0:T(8,128)(2,1)} custom-call(bf16[256,192]{1,0:T(8,128)(2,1)} %fusion.2.pick_ref, bf16[2,96,3072]{2,1,0:T(8,128)(2,1)} %rows_ref.1), custom_call_target="tpu_custom_call" | custom-call | tf_op jit(solution)/shard_map/gather_rows/pallas_call | solution.py:88
  8.2 7.1 %all-to-all-start.1 = ((bf16[32,8,3072]{2,1,0:T(8,128)(2,1)}), bf16[32,8,3072]{2,1,0:T(8,128)(2,1)S(1)}, u32[]{:S(2)}, u32[]{:S(2)}) async-start(bf16[32,8,3072]{2,1,0:T(8,128)(2,1)} %bitcast.12), calls=%async_computation.1 | async-start | bytes 3145728 | tf_op jit(solution)/shard_map/all_to_all | solution.py:435
  15.3 0.0 copy-done
  15.3 0.0 copy-start.3
  15.3 0.7 fusion.11
  16.1 5.0 %collective-permute-start.4 = (bf16[2,64,64]{2,1,0:T(8,128)(2,1)}, bf16[2,64,64]{2,1,0:T(8,128)(2,1)}, u32[]{:S(2)}, u32[]{:S(2)}) collective-permute-start(bf16[2,64,64]{2,1,0:T(8,128)(2,1)} %get-tuple-element.24), channel_id=1, source_target_pairs={{0,5},{1,6},{2,7},{4,9},{5,10},{6,11},{8,13},{9,14},{10,15},{12,17... | collective-permute-start | bytes 49160 | tf_op jit(solution)/shard_map/ppermute | solution.py:36
  21.1 1.3 %collective-permute-start.5 = (bf16[2,64,64]{2,1,0:T(8,128)(2,1)}, bf16[2,64,64]{2,1,0:T(8,128)(2,1)}, u32[]{:S(2)}, u32[]{:S(2)}) collective-permute-start(bf16[2,64,64]{2,1,0:T(8,128)(2,1)} %get-tuple-element.23), channel_id=1, source_target_pairs={{1,4},{2,5},{3,6},{5,8},{6,9},{7,10},{9,12},{10,13},{11,14},{13,16... | collective-permute-start | bytes 49160 | tf_op jit(solution)/shard_map/ppermute | solution.py:36
  22.4 0.0 slice-start
  22.4 5.6 %collective-permute-start.6 = (bf16[2,64,64]{2,1,0:T(8,128)(2,1)}, bf16[2,64,64]{2,1,0:T(8,128)(2,1)}, u32[]{:S(2)}, u32[]{:S(2)}) collective-permute-start(bf16[2,64,64]{2,1,0:T(8,128)(2,1)} %get-tuple-element.22), channel_id=1, source_target_pairs={{4,1},{5,2},{6,3},{8,5},{9,6},{10,7},{12,9},{13,10},{14,11},{16,13... | collective-permute-start | bytes 49160 | tf_op jit(solution)/shard_map/ppermute | solution.py:36
  28.0 1.4 %fusion.12 = (bf16[2,64,3072]{2,1,0:T(8,128)(2,1)}, bf16[2,64,3072]{2,1,0:T(8,128)(2,1)}) fusion(bf16[2,96,3072]{2,1,0:T(8,128)(2,1)S(1)} %copy-done), kind=kLoop, calls=%fused_computation.49 | loop fusion | bytes 3145728 | tf_op jit(solution)/shard_map/slice | solution.py:395
  29.4 0.0 copy-start.4
  29.4 2.6 %collective-permute-start = (bf16[2,64,3072]{2,1,0:T(8,128)(2,1)}, bf16[2,64,3072]{2,1,0:T(8,128)(2,1)}, u32[]{:S(2)}, u32[]{:S(2)}) collective-permute-start(bf16[2,64,3072]{2,1,0:T(8,128)(2,1)} %get-tuple-element.26), channel_id=1, source_target_pairs={{0,4},{1,5},{2,6},{3,7},{4,8},{5,9},{6,10},{7,11},{8,12},{9,13},{1... | collective-permute-start | bytes 2359304 | tf_op jit(solution)/shard_map/ppermute | solution.py:36
  32.0 2.7 %collective-permute-start.1 = (bf16[2,64,3072]{2,1,0:T(8,128)(2,1)}, bf16[2,64,3072]{2,1,0:T(8,128)(2,1)}, u32[]{:S(2)}, u32[]{:S(2)}) collective-permute-start(bf16[2,64,3072]{2,1,0:T(8,128)(2,1)} %get-tuple-element.25), channel_id=1, source_target_pairs={{4,0},{5,1},{6,2},{7,3},{8,4},{9,5},{10,6},{11,7},{12,8},{13,9},{1... | collective-permute-start | bytes 2359304 | tf_op jit(solution)/shard_map/ppermute | solution.py:36
  34.8 0.0 copy-done.3
  34.8 0.1 select_reduce_fusion.1
  35.0 0.1 select_n.73
  35.1 0.8 fusion.1.pick_ref
  35.8 1.4 %fusion.6 = s32[12288]{0:T(1024)} fusion(s32[12288]{0:T(1024)} %param.18), kind=kLoop, calls=%fused_computation.21 | loop fusion | flops 135168 | bytes 98304 | tf_op jit(solution)/shard_map/add | solution.py:453
  37.3 0.0 slice-done
  37.3 0.7 pad_maximum_fusion
  38.0 3.7 %collective-permute-done.4.top_left = bf16[2,64,64]{2,1,0:T(8,128)(2,1)} collective-permute-done((bf16[2,64,64]{2,1,0:T(8,128)(2,1)}, bf16[2,64,64]{2,1,0:T(8,128)(2,1)}, u32[]{:S(2)}, u32[]{:S(2)}) %collective-permute-start.4) | collective-permute-done | bytes 16416 | tf_op jit(solution)/shard_map/ppermute | solution.py:36
  41.7 1.3 %collective-permute-start.7 = (bf16[2,64,64]{2,1,0:T(8,128)(2,1)}, bf16[2,64,64]{2,1,0:T(8,128)(2,1)S(1)}, u32[]{:S(2)}, u32[]{:S(2)}) collective-permute-start(bf16[2,64,64]{2,1,0:T(8,128)(2,1)} %get-tuple-element.21), channel_id=1, source_target_pairs={{5,0},{6,1},{7,2},{9,4},{10,5},{11,6},{13,8},{14,9},{15,10},{17,12... | collective-permute-start | bytes 49160 | tf_op jit(solution)/shard_map/ppermute | solution.py:36
  43.0 0.0 collective-permute-done.5.top_right
  43.0 12.5 %collective-permute-start.2 = (bf16[2,160,64]{2,1,0:T(8,128)(2,1)}, bf16[2,160,64]{2,1,0:T(8,128)(2,1)S(1)}, u32[]{:S(2)}, u32[]{:S(2)}) collective-permute-start(bf16[2,160,64]{2,1,0:T(8,128)(2,1)} %get-tuple-element.20), channel_id=1, source_target_pairs={{0,1},{1,2},{2,3},{4,5},{5,6},{6,7},{8,9},{9,10},{10,11},{12,13},{... | collective-permute-start | bytes 122888 | tf_op jit(solution)/shard_map/ppermute | solution.py:36
  55.5 0.0 collective-permute-done.6.low_left
  55.5 1.3 %collective-permute-start.3 = (bf16[2,160,64]{2,1,0:T(8,128)(2,1)}, bf16[2,160,64]{2,1,0:T(8,128)(2,1)S(1)}, u32[]{:S(2)}, u32[]{:S(2)}) collective-permute-start(bf16[2,160,64]{2,1,0:T(8,128)(2,1)} %get-tuple-element.19), channel_id=1, source_target_pairs={{1,0},{2,1},{3,2},{5,4},{6,5},{7,6},{9,8},{10,9},{11,10},{13,12},{... | collective-permute-start | bytes 122888 | tf_op jit(solution)/shard_map/ppermute | solution.py:36
  56.8 0.0 copy-done.4
  56.8 0.6 pad_convert_fusion.base_ref
  57.4 10.1 %build_bands.1.band_ref = bf16[96,256,128]{2,1,0:T(8,128)(2,1)} custom-call(s32[1,12288]{1,0:T(1,128)} %bitcast.14, bf16[8,12288]{1,0:T(8,128)(2,1)} %taps_ref.1), custom_call_target="tpu_custom_call" | custom-call | flops 100663296 | bytes 6291456 | tf_op jit(solution)/shard_map/build_bands/pallas_call | solution.py:117
  67.5 0.0 collective-permute-done.7.low_right
  67.5 0.0 copy-start.7
  67.5 0.0 collective-permute-done.2.left
  67.5 0.0 copy-start.5
  67.5 0.0 collective-permute-done.3.right
  67.6 0.0 copy-start.6
  67.6 0.0 collective-permute-done.sec_top
  67.6 0.0 collective-permute-done.1.sec_low
  67.6 0.5 copy-done.7
  68.1 0.1 copy-done.5
  68.2 0.0 copy-done.6
  68.2 11.0 %estimate_shifts.1 = (f32[2,128]{1,0:T(2,128)}, f32[32,128]{1,0:T(8,128)}) custom-call(s32[2,96]{1,0:T(2,128)} %bitcast.17, bf16[2,96,3072]{2,1,0:T(8,128)(2,1)} %ref_ref.1, bf16[2,96,3072]{2,1,0:T(8,128)(2,1)} %rows_ref.1, bf16[2,64,3072]{2,1,0:T(8,128)(2,1)} %collective-permute-done.sec_top, bf16[2,64,3072]{2,1,0:T(8,128)(2,1)} %collective-permute-done.1.sec_low, ...), custom_call_target="tpu_custom_call" | custom-call | flops 10000000000 | bytes 8000000 | tf_op jit(solution)/shard_map/estimate_shifts/pallas_call | solution.py:260
  79.2 0.0 all-to-all-done.1
  79.2 0.0 copy-start.1
  79.2 8.8 %all-to-all-start = ((f32[32,1,128]{2,1,0:T(1,128)}), f32[32,1,128]{2,1,0:T(1,128)S(1)}, u32[]{:S(2)}, u32[]{:S(2)}) async-start(f32[32,1,128]{2,1,0:T(1,128)} %bitcast.16), calls=%async_computation | async-start | bytes 32768 | tf_op jit(solution)/shard_map/all_to_all | solution.py:444
  88.0 0.0 copy-done.1
  88.0 7.5 %resample.1.lines_ref = f32[2,32,12288]{2,1,0:T(8,128)} custom-call(bf16[256,256]{1,0:T(8,128)(2,1)} %fusion.1.pick_ref, bf16[256,3072]{1,0:T(8,128)(2,1)} %bitcast.13, bf16[96,256,128]{2,1,0:T(8,128)(2,1)} %build_bands.1.band_ref), custom_call_target="tpu_custom_call" | custom-call | flops 6000000000 | bytes 12000000 | tf_op jit(solution)/shard_map/resample/pallas_call | solution.py:310
  95.5 0.0 all-to-all-done
  95.5 0.0 copy-start.2
  95.5 0.7 broadcast_in_dim.90.tile_ref
  96.1 0.0 copy-done.2
  96.1 4.6 %rotate.1 = bf16[2,32,12288]{2,1,0:T(8,128)(2,1)} custom-call(s32[32,128]{1,0:T(8,128)} %broadcast_in_dim.90.tile_ref, f32[32,128]{1,0:T(8,128)} %bitcast.15, f32[2,32,12288]{2,1,0:T(8,128)} %resample.1.lines_ref), custom_call_target="tpu_custom_call" | custom-call | tf_op jit(solution)/shard_map/rotate/pallas_call | solution.py:361
  (9 shorter events, 0.1 us)
Async XLA Ops:
  4.5 10.8 %copy-start = (bf16[2,96,3072]{2,1,0:T(8,128)(2,1)S(1)}, bf16[2,96,3072]{2,1,0:T(8,128)(2,1)}, u32[]{:S(2)}) copy-start(bf16[2,96,3072]{2,1,0:T(8,128)(2,1)} %rows_ref.1) | copy-start | bytes 3538948
  8.2 71.0 %all-to-all-start.1 = ((bf16[32,8,3072]{2,1,0:T(8,128)(2,1)}), bf16[32,8,3072]{2,1,0:T(8,128)(2,1)S(1)}, u32[]{:S(2)}, u32[]{:S(2)}) async-start(bf16[32,8,3072]{2,1,0:T(8,128)(2,1)} %bitcast.12), calls=%async_computation.1 | async-start | bytes 3145728 | tf_op jit(solution)/shard_map/all_to_all | solution.py:435
  15.3 19.5 %copy-start.3 = (s32[768]{0:T(1024)S(1)}, s32[768]{0:T(1024)}, u32[]{:S(2)}) copy-start(s32[768]{0:T(1024)} %param.17) | copy-start | bytes 9220
  16.1 25.7 %collective-permute-start.4 = (bf16[2,64,64]{2,1,0:T(8,128)(2,1)}, bf16[2,64,64]{2,1,0:T(8,128)(2,1)}, u32[]{:S(2)}, u32[]{:S(2)}) collective-permute-start(bf16[2,64,64]{2,1,0:T(8,128)(2,1)} %get-tuple-element.24), channel_id=1, source_target_pairs={{0,5},{1,6},{2,7},{4,9},{5,10},{6,11},{8,13},{9,14},{10,15},{12,17... | collective-permute-start | bytes 49160 | tf_op jit(solution)/shard_map/ppermute | solution.py:36
  21.1 21.9 %collective-permute-start.5 = (bf16[2,64,64]{2,1,0:T(8,128)(2,1)}, bf16[2,64,64]{2,1,0:T(8,128)(2,1)}, u32[]{:S(2)}, u32[]{:S(2)}) collective-permute-start(bf16[2,64,64]{2,1,0:T(8,128)(2,1)} %get-tuple-element.23), channel_id=1, source_target_pairs={{1,4},{2,5},{3,6},{5,8},{6,9},{7,10},{9,12},{10,13},{11,14},{13,16... | collective-permute-start | bytes 49160 | tf_op jit(solution)/shard_map/ppermute | solution.py:36
  22.4 14.9 %slice-start = ((bf16[2,96,3072]{2,1,0:T(8,128)(2,1)}), bf16[2,64,3072]{2,1,0:T(8,128)(2,1)S(1)}, s32[]{:S(2)}) async-start(bf16[2,96,3072]{2,1,0:T(8,128)(2,1)} %ref_ref.1), calls=%async_computation.2 | async-start | bytes 1572864 | tf_op jit(solution)/shard_map/slice | solution.py:398
  22.4 33.1 %collective-permute-start.6 = (bf16[2,64,64]{2,1,0:T(8,128)(2,1)}, bf16[2,64,64]{2,1,0:T(8,128)(2,1)}, u32[]{:S(2)}, u32[]{:S(2)}) collective-permute-start(bf16[2,64,64]{2,1,0:T(8,128)(2,1)} %get-tuple-element.22), channel_id=1, source_target_pairs={{4,1},{5,2},{6,3},{8,5},{9,6},{10,7},{12,9},{13,10},{14,11},{16,13... | collective-permute-start | bytes 49160 | tf_op jit(solution)/shard_map/ppermute | solution.py:36
  29.4 27.4 %copy-start.4 = (s32[2,1,96]{2,1,0:T(1,128)S(1)}, s32[2,1,96]{2,1,0:T(1,128)}, u32[]{:S(2)}) copy-start(s32[2,1,96]{2,1,0:T(1,128)} %param.15) | copy-start | bytes 2308
  29.4 38.2 %collective-permute-start = (bf16[2,64,3072]{2,1,0:T(8,128)(2,1)}, bf16[2,64,3072]{2,1,0:T(8,128)(2,1)}, u32[]{:S(2)}, u32[]{:S(2)}) collective-permute-start(bf16[2,64,3072]{2,1,0:T(8,128)(2,1)} %get-tuple-element.26), channel_id=1, source_target_pairs={{0,4},{1,5},{2,6},{3,7},{4,8},{5,9},{6,10},{7,11},{8,12},{9,13},{1... | collective-permute-start | bytes 2359304 | tf_op jit(solution)/shard_map/ppermute | solution.py:36
  32.0 35.5 %collective-permute-start.1 = (bf16[2,64,3072]{2,1,0:T(8,128)(2,1)}, bf16[2,64,3072]{2,1,0:T(8,128)(2,1)}, u32[]{:S(2)}, u32[]{:S(2)}) collective-permute-start(bf16[2,64,3072]{2,1,0:T(8,128)(2,1)} %get-tuple-element.25), channel_id=1, source_target_pairs={{4,0},{5,1},{6,2},{7,3},{8,4},{9,5},{10,6},{11,7},{12,8},{13,9},{1... | collective-permute-start | bytes 2359304 | tf_op jit(solution)/shard_map/ppermute | solution.py:36
  41.7 25.8 %collective-permute-start.7 = (bf16[2,64,64]{2,1,0:T(8,128)(2,1)}, bf16[2,64,64]{2,1,0:T(8,128)(2,1)S(1)}, u32[]{:S(2)}, u32[]{:S(2)}) collective-permute-start(bf16[2,64,64]{2,1,0:T(8,128)(2,1)} %get-tuple-element.21), channel_id=1, source_target_pairs={{5,0},{6,1},{7,2},{9,4},{10,5},{11,6},{13,8},{14,9},{15,10},{17,12... | collective-permute-start | bytes 49160 | tf_op jit(solution)/shard_map/ppermute | solution.py:36
  43.0 24.5 %collective-permute-start.2 = (bf16[2,160,64]{2,1,0:T(8,128)(2,1)}, bf16[2,160,64]{2,1,0:T(8,128)(2,1)S(1)}, u32[]{:S(2)}, u32[]{:S(2)}) collective-permute-start(bf16[2,160,64]{2,1,0:T(8,128)(2,1)} %get-tuple-element.20), channel_id=1, source_target_pairs={{0,1},{1,2},{2,3},{4,5},{5,6},{6,7},{8,9},{9,10},{10,11},{12,13},{... | collective-permute-start | bytes 122888 | tf_op jit(solution)/shard_map/ppermute | solution.py:36
  55.5 12.0 %collective-permute-start.3 = (bf16[2,160,64]{2,1,0:T(8,128)(2,1)}, bf16[2,160,64]{2,1,0:T(8,128)(2,1)S(1)}, u32[]{:S(2)}, u32[]{:S(2)}) collective-permute-start(bf16[2,160,64]{2,1,0:T(8,128)(2,1)} %get-tuple-element.19), channel_id=1, source_target_pairs={{1,0},{2,1},{3,2},{5,4},{6,5},{7,6},{9,8},{10,9},{11,10},{13,12},{... | collective-permute-start | bytes 122888 | tf_op jit(solution)/shard_map/ppermute | solution.py:36
  67.5 0.6 copy-start.7
  67.5 0.6 copy-start.5
  67.6 0.6 copy-start.6
  79.2 8.8 %copy-start.1 = (bf16[32,8,3072]{2,1,0:T(8,128)(2,1)}, bf16[32,8,3072]{2,1,0:T(8,128)(2,1)S(1)}, u32[]{:S(2)}) copy-start(bf16[32,8,3072]{2,1,0:T(8,128)(2,1)S(1)} %all-to-all-done.1) | copy-start | bytes 4718596
  79.2 16.3 %all-to-all-start = ((f32[32,1,128]{2,1,0:T(1,128)}), f32[32,1,128]{2,1,0:T(1,128)S(1)}, u32[]{:S(2)}, u32[]{:S(2)}) async-start(f32[32,1,128]{2,1,0:T(1,128)} %bitcast.16), calls=%async_computation | async-start | bytes 32768 | tf_op jit(solution)/shard_map/all_to_all | solution.py:444
  95.5 0.7 copy-start.2
